TPU v7x, 256 devices: a whole 4x4x8 slice. The times are simulated.
256 devices in a mesh: seq: 32 (over x, y, core), ch: 8 (over z).
Axes of the slice: x: 4, y: 4, z: 8, core: 2. Of those that a mesh axis runs over, the one named last changes fastest.
Arguments:
- token_ids: int32 [32768], P('seq'), may hold values from 0 to 511
- embedding: bfloat16 [4096, 512], P('ch'), may hold values from -26 to 26
- projected: bfloat16 [3, 4096, 512], P(None, 'ch'), may hold values from -6 to 6
- short_taps: float32 [7, 3, 4096], P(None, None, 'ch'), may hold values from -2 to 2
- long_filter: bfloat16 [4096, 32768], P('ch', 'seq'), may hold values from -1.6 to 1.6
- skip_gain: float32 [4096], P('ch'), may hold values from -3 to 3
Outputs:
- mixed: bfloat16 [4096, 32768], P('ch', 'seq')
All inputs are finite; a program needn't handle non-finite values.
Results may differ from a plain program's by a relative error of at most 0.0075.
Values may be sent and summed in bfloat16 or wider, within the bound.
No kernel may reach another device: no remote copies, remote signals or barrier semaphores. Data moves between devices by JAX's collectives and lax.ppermute only.
A program may use at most 128 MiB of HBM per device.

v0:
```python
import math

import jax
import jax.numpy as jnp
from jax import lax
from jax.sharding import PartitionSpec as P

MIXER_CHANNELS = 4096


EPSILON = 1e-06
PRECISE = lax.Precision.HIGH


def passed_along(value, axis, by):
    size = lax.axis_size(axis)
    pairs = [(i, i + by) for i in range(size) if 0 <= i + by < size]
    return lax.ppermute(value, axis, pairs)


def short_conv(padded, weights):
    tap_count = weights.shape[0]
    filter_extent = padded.shape[2] - (tap_count - 1)
    acc_sum = jnp.zeros(padded.shape[:2] + (filter_extent,), jnp.float32)
    for offset in range(tap_count):
        begin = tap_count - 1 - offset
        acc_sum = acc_sum + weights[offset][:, :, None] * padded[
            :, :, begin : begin + filter_extent
        ].astype(jnp.float32)
    return acc_sum


def cos_sin(left, right, modulus):
    index_grid = left[:, None] * right[None, :] % modulus
    angles = index_grid.astype(jnp.float32) * (2.0 * math.pi / modulus)
    return (jnp.cos(angles), jnp.sin(angles))


def long_conv(gated_rows, filter_rows):
    group_size, filter_extent = gated_rows.shape
    fft_length = 2 * filter_extent
    first_len = 2
    while fft_length % (first_len * 2) == 0 and first_len * first_len * 4 <= fft_length:
        first_len = first_len * 2
    second_len = fft_length // first_len
    half_rows = first_len // 2
    frequency = jnp.arange(first_len, dtype=jnp.int32)
    position = jnp.arange(half_rows, dtype=jnp.int32)
    inner = jnp.arange(second_len, dtype=jnp.int32)
    cos_first, sin_first = cos_sin(frequency, position, first_len)
    cos_twist, sin_twist = cos_sin(frequency, inner, fft_length)
    cos_second, sin_second = cos_sin(inner, inner, second_len)

    def along_last(left, table):
        return jnp.einsum("gkb,bm->gkm", left, table, precision=PRECISE)

    def forward(signal):
        shaped = signal.astype(jnp.float32).reshape(group_size, half_rows, second_len)
        real_a = jnp.einsum("ka,gab->gkb", cos_first, shaped, precision=PRECISE)
        imag_a = -jnp.einsum("ka,gab->gkb", sin_first, shaped, precision=PRECISE)
        real_b = real_a * cos_twist + imag_a * sin_twist
        imag_b = imag_a * cos_twist - real_a * sin_twist
        real_c = along_last(real_b, cos_second) + along_last(imag_b, sin_second)
        imag_c = along_last(imag_b, cos_second) - along_last(real_b, sin_second)
        return (real_c, imag_c)

    real_z, imag_z = forward(gated_rows)
    real_h, imag_h = forward(filter_rows)
    real_y = real_z * real_h - imag_z * imag_h
    imag_y = real_z * imag_h + imag_z * real_h
    real_p = along_last(real_y, cos_second) - along_last(imag_y, sin_second)
    imag_p = along_last(imag_y, cos_second) + along_last(real_y, sin_second)
    real_q = real_p * cos_twist - imag_p * sin_twist
    imag_q = imag_p * cos_twist + real_p * sin_twist
    result = jnp.einsum("ka,gkb->gab", cos_first, real_q, precision=PRECISE) - jnp.einsum(
        "ka,gkb->gab", sin_first, imag_q, precision=PRECISE
    )
    return result.reshape(group_size, filter_extent) / fft_length


def shards(token_ids, embedding, projected, short_taps, long_filter, skip_gain):
    seq_count = lax.axis_size("seq")
    seq_index = lax.axis_index("seq")
    local_ch, vocab = embedding.shape
    tokens = token_ids.shape[0]
    tap_count = short_taps.shape[0]
    group_size = local_ch // seq_count
    filter_cols = lax.all_to_all(long_filter, "seq", split_axis=0, concat_axis=1, tiled=True)
    values = embedding.astype(jnp.float32)
    squares = lax.psum(jnp.sum(values * values, axis=0), "ch")
    vocab_scale = 1.0 / jnp.sqrt(squares / MIXER_CHANNELS + EPSILON)
    row_table = projected.reshape(3 * local_ch, vocab)
    onehot = jnp.arange(vocab, dtype=jnp.int32)[:, None] == token_ids[None, :]
    looked_up = jnp.dot(row_table, onehot.astype(jnp.bfloat16), preferred_element_type=jnp.float32)
    picked = jnp.dot(vocab_scale[None, :], onehot.astype(jnp.float32), precision=PRECISE)
    streams = (looked_up * picked).astype(jnp.bfloat16).reshape(3, local_ch, tokens)
    earlier = passed_along(streams[:, :, tokens - (tap_count - 1) :], "seq", 1)
    conv_out = short_conv(jnp.concatenate([earlier, streams], axis=2), short_taps)
    first_stream = conv_out[0]
    gated_rows = (conv_out[1] * conv_out[2]).astype(jnp.bfloat16)
    gated_cols = lax.all_to_all(gated_rows, "seq", split_axis=0, concat_axis=1, tiled=True)
    skip_rows = lax.dynamic_slice_in_dim(skip_gain, seq_index * group_size, group_size)
    convolved = long_conv(gated_cols, filter_cols)
    long_out = (convolved + skip_rows[:, None] * gated_cols.astype(jnp.float32)).astype(
        jnp.bfloat16
    )
    returned = lax.all_to_all(long_out, "seq", split_axis=1, concat_axis=0, tiled=True)
    return (first_stream * returned.astype(jnp.float32)).astype(jnp.bfloat16)


def solution(mesh):
    placed = (
        P("seq"),
        P("ch", None),
        P(None, "ch", None),
        P(None, None, "ch"),
        P("ch", "seq"),
        P("ch"),
    )
    return jax.shard_map(
        shards, mesh=mesh, in_specs=placed, out_specs=P("ch", "seq"), check_vma=False
    )
```

profile of v0, /device:TPU:1, one launch (start us, length us, event | category | flops | bytes accessed | tf_op | source)
XLA Modules:
  0.0 195.5 jit_solution(2268663443835254987)
XLA Ops:
  0.0 0.0 copy-start
  0.0 8.8 %all-to-all-start.1 = ((bf16[32,16,1024]{2,1,0:T(8,128)(2,1)}), bf16[32,16,1024]{2,1,0:T(8,128)(2,1)}, u32[]{:S(2)}, u32[]{:S(2)}) async-start(bf16[32,16,1024]{2,1,0:T(8,128)(2,1)} %bitcast.137), calls=%async_computation.1 | async-start | bytes 2097152 | tf_op jit(solution)/shard_map/all_to_all | solution.py:88
  8.8 1.2 multiply_reduce_fusion
  10.0 17.4 %psum.7 = f32[512]{0:T(512)S(1)} all-reduce(f32[512]{0:T(512)S(1)} %multiply_reduce_fusion), channel_id=1, replica_groups=mesh['seq'=32,'ch'=8] {'ch'}, use_global_device_ids=true, to_apply=%region_1.0 | all-reduce | flops 512 | bytes 4096 | tf_op jit(solution)/shard_map/psum | solution.py:90
  27.4 1.3 fusion.37
  28.7 0.0 copy-done
  28.7 4.4 %fusion.18 = bf16[1536,1024]{0,1:T(8,128)(2,1)} fusion(bf16[1536,512]{1,0:T(8,128)(2,1)S(1)} %bitcast.133, f32[1024]{0:T(1024)S(1)} %bitcast.140, s32[1024]{0:T(1024)} %param.6), kind=kOutput, calls=%fused_computation.33 | convolution fusion | flops 1614807040 | bytes 4726784 | tf_op jit(solution)/shard_map/dot_general | solution.py:94
  33.1 0.0 copy-start.7
  33.1 3.2 %copy.38 = bf16[1536,1024]{1,0:T(8,128)(2,1)S(1)} copy(bf16[1536,1024]{0,1:T(8,128)(2,1)} %fusion.18) | data formatting | bytes 6291456 | tf_op jit(solution)/shard_map/convert_element_type | solution.py:96
  36.3 0.9 slice.68
  37.2 6.1 %collective-permute-start = (bf16[3,512,6]{2,1,0:T(8,128)(2,1)}, bf16[3,512,6]{2,1,0:T(8,128)(2,1)}, u32[]{:S(2)}, u32[]{:S(2)}) collective-permute-start(bf16[3,512,6]{2,1,0:T(8,128)(2,1)} %slice.68), channel_id=1, source_target_pairs={{0,8},{8,16},{16,24},{24,32},{32,40},{40,48},{48,56},{56,64},{64,7... | collective-permute-start | bytes 55304 | tf_op jit(solution)/shard_map/ppermute | solution.py:18
  43.3 0.0 copy-done.7
  43.4 1.8 fusion.102
  45.2 1.1 copy.43
  46.3 1.8 copy.41
  48.1 0.8 dynamic_slice.3
  48.9 0.0 collective-permute-done
  48.9 11.8 %multiply_add_fusion = f32[3,512,1024]{2,1,0:T(8,128)} fusion(bf16[3,512,1024]{2,1,0:T(8,128)(2,1)S(1)} %bitcast.135, bf16[3,512,6]{2,1,0:T(8,128)(2,1)} %collective-permute-done, f32[3,512]{1,0:T(4,128)S(1)} %get-tuple-element.14, f32[3,512]{1,0:T(4,128)S(1)} %get-tuple-element.15, f32[3,512]{1,0:T(4,128)S(1)} %get-tuple-element.16, ...), kind=kLoop, calls=%fused_computation.5 | loop fusion | flops 59768832 | bytes 9498624 | tf_op jit(solution)/shard_map/add | solution.py:27
  60.6 3.5 %fusion.30 = bf16[1,512,1024]{2,1,0:T(8,128)(2,1)} fusion(f32[3,512,1024]{2,1,0:T(8,128)} %multiply_add_fusion), kind=kLoop, calls=%fused_computation.50 | loop fusion | flops 1048576 | bytes 5242880 | tf_op jit(solution)/shard_map/convert_element_type | solution.py:100
  64.1 0.0 all-to-all-done.1
  64.2 7.7 %all-to-all-start = ((bf16[32,16,1024]{2,1,0:T(8,128)(2,1)}), bf16[32,16,1024]{2,1,0:T(8,128)(2,1)S(1)}, u32[]{:S(2)}, u32[]{:S(2)}) async-start(bf16[32,16,1024]{2,1,0:T(8,128)(2,1)} %bitcast.6), calls=%async_computation | async-start | bytes 2097152 | tf_op jit(solution)/shard_map/all_to_all | solution.py:101
  71.9 1.8 copy.46
  73.7 0.9 reshape.90
  74.6 0.0 copy-start.3
  74.6 0.0 copy-start.4
  74.6 1.7 fusion.79
  76.3 1.7 fusion.84
  78.0 0.0 copy-done.3
  78.1 0.0 copy-done.4
  78.1 3.1 %fusion = f32[16,256,256]{2,1,0:T(8,128)S(1)} fusion(f32[256,16,256]{2,0,1:T(8,128)S(1)} %fusion.84, f32[256,16,256]{2,0,1:T(8,128)S(1)} %fusion.79, f32[256,256]{1,0:T(8,128)S(1)} %copy-done.3, f32[256,256]{1,0:T(8,128)S(1)} %copy-done.4), kind=kOutput, calls=%fused_computation.7 | convolution fusion | flops 1615724544 | bytes 13107200 | tf_op jit(solution)/shard_map/gkb,bm->gkm/dot_general | solution.py:55
  81.1 5.1 %fusion.27 = f32[16,256,256]{2,1,0:T(8,128)} fusion(f32[16,256,256]{2,1,0:T(8,128)S(1)} %fusion, f32[256,16,256]{2,0,1:T(8,128)S(1)} %fusion.84, f32[256,16,256]{2,0,1:T(8,128)S(1)} %fusion.79, f32[256,256]{1,0:T(8,128)S(1)} %copy-done.3, f32[256,256]{1,0:T(8,128)S(1)} %copy-done.4), kind=kOutput, calls=%fused_computation.44 | convolution fusion | flops 1616773120 | bytes 17301504 | tf_op jit(solution)/shard_map/gkb,bm->gkm/dot_general | solution.py:55
  86.3 15.0 %fusion.2 = f32[16,256,256]{2,1,0:T(8,128)S(1)} fusion(f32[256,16,256]{2,0,1:T(8,128)S(1)} %fusion.84, f32[256,16,256]{2,0,1:T(8,128)S(1)} %fusion.79, f32[256,256]{1,0:T(8,128)S(1)} %copy-done.3, f32[256,256]{1,0:T(8,128)S(1)} %copy-done.4), kind=kOutput, calls=%fused_computation.9 | convolution fusion | flops 1615724544 | bytes 13107200 | tf_op jit(solution)/shard_map/gkb,bm->gkm/dot_general | solution.py:55
  101.3 5.1 %fusion.24 = f32[16,256,256]{2,1,0:T(8,128)} fusion(f32[16,256,256]{2,1,0:T(8,128)S(1)} %fusion.2, f32[256,16,256]{2,0,1:T(8,128)S(1)} %fusion.84, f32[256,16,256]{2,0,1:T(8,128)S(1)} %fusion.79, f32[256,256]{1,0:T(8,128)S(1)} %copy-done.3, f32[256,256]{1,0:T(8,128)S(1)} %copy-done.4), kind=kOutput, calls=%fused_computation.43 | convolution fusion | flops 1616773120 | bytes 17301504 | tf_op jit(solution)/shard_map/gkb,bm->gkm/dot_general | solution.py:55
  106.4 0.0 all-to-all-done
  106.4 0.0 copy-start.5
  106.4 0.6 copy.82
  107.0 0.7 reshape.89
  107.6 0.0 copy-start.2
  107.6 1.7 fusion.81
  109.4 0.0 copy-done.5
  109.4 1.7 fusion.86
  111.2 0.0 copy-done.2
  111.2 6.5 %fusion.44 = f32[16,256,256]{2,1,0:T(8,128)} fusion(f32[16,256,256]{2,1,0:T(8,128)S(1)} %fusion.86, f32[16,256,256]{2,1,0:T(8,128)S(1)} %fusion.81, f32[256,256]{0,1:T(8,128)S(1)} %copy.43, f32[256,256]{0,1:T(8,128)S(1)} %copy-done.2), kind=kOutput, calls=%fused_computation.67 | convolution fusion | flops 1615724544 | bytes 13107200 | tf_op jit(solution)/shard_map/gkb,bm->gkm/dot_general | solution.py:55
  117.7 5.0 %fusion.48 = f32[16,256,256]{2,1,0:T(8,128)S(1)} fusion(f32[16,256,256]{2,1,0:T(8,128)S(1)} %fusion.86, f32[16,256,256]{2,1,0:T(8,128)S(1)} %fusion.81, f32[256,256]{0,1:T(8,128)S(1)} %copy.43, f32[256,256]{0,1:T(8,128)S(1)} %copy-done.2), kind=kOutput, calls=%fused_computation.68 | convolution fusion | flops 1615724544 | bytes 13107200 | tf_op jit(solution)/shard_map/gkb,bm->gkm/dot_general | solution.py:55
  122.6 6.6 %convolution_add_fusion.1 = f32[16,256,256]{2,1,0:T(8,128)} fusion(f32[16,256,256]{2,1,0:T(8,128)S(1)} %fusion.48, f32[16,256,256]{2,1,0:T(8,128)S(1)} %fusion.86, f32[16,256,256]{2,1,0:T(8,128)S(1)} %fusion.81, f32[256,256]{0,1:T(8,128)S(1)} %copy.43, f32[256,256]{0,1:T(8,128)S(1)} %copy-done.2), kind=kOutput, calls=%fused_computation.48 | convolution fusion | flops 1616773120 | bytes 17301504 | tf_op jit(solution)/shard_map/gkb,bm->gkm/dot_general | solution.py:55
  129.2 11.9 %multiply_add_fusion.1 = (f32[16,256,256]{2,1,0:T(8,128)S(1)}, f32[16,256,256]{2,1,0:T(8,128)S(1)}) fusion(f32[16,256,256]{2,1,0:T(8,128)} %fusion.24, f32[16,256,256]{2,1,0:T(8,128)} %convolution_add_fusion.1, f32[16,256,256]{2,1,0:T(8,128)} %fusion.27, f32[16,256,256]{2,1,0:T(8,128)} %fusion.44, f32[16,256,256]{2,1,0:T(8,128)S(1)} %fusion.86, ...), kind=kOutput, calls=%fused_computation.29 | convolution fusion | flops 1623064576 | bytes 34078720 | tf_op jit(solution)/shard_map/gkb,bm->gkm/dot_general | solution.py:55
  141.1 2.8 %fusion.60 = f32[16,256,256]{1,2,0:T(8,128)S(1)} fusion(f32[16,256,256]{2,1,0:T(8,128)S(1)} %get-tuple-element.5), kind=kOutput, calls=%fused_computation.84 | convolution fusion | flops 1611530240 | bytes 8388608 | tf_op jit(solution)/shard_map/gkb,bm->gkm/dot_general | solution.py:55
  143.9 2.8 %fusion.62 = f32[16,256,256]{1,2,0:T(8,128)S(1)} fusion(f32[16,256,256]{2,1,0:T(8,128)S(1)} %get-tuple-element.6), kind=kOutput, calls=%fused_computation.86 | convolution fusion | flops 1611530240 | bytes 8388608 | tf_op jit(solution)/shard_map/gkb,bm->gkm/dot_general | solution.py:55
  146.8 2.9 %convolution_add_fusion = f32[16,256,256]{1,2,0:T(8,128)S(1)} fusion(f32[16,256,256]{1,2,0:T(8,128)S(1)} %fusion.60, f32[16,256,256]{2,1,0:T(8,128)S(1)} %get-tuple-element.6), kind=kOutput, calls=%fused_computation.45 | convolution fusion | flops 1612578816 | bytes 12582912 | tf_op jit(solution)/shard_map/gkb,bm->gkm/dot_general | solution.py:55
  149.7 2.9 %convolution_subtract_fusion = f32[16,256,256]{1,2,0:T(8,128)S(1)} fusion(f32[16,256,256]{1,2,0:T(8,128)S(1)} %fusion.62, f32[16,256,256]{2,1,0:T(8,128)S(1)} %get-tuple-element.5), kind=kOutput, calls=%fused_computation.46 | convolution fusion | flops 1612578816 | bytes 12582912 | tf_op jit(solution)/shard_map/gkb,bm->gkm/dot_general | solution.py:55
  152.5 2.8 %fusion.10 = f32[16,256,128]{2,1,0:T(8,128)S(1)} fusion(f32[16,256,256]{1,2,0:T(8,128)S(1)} %convolution_subtract_fusion, f32[16,256,256]{1,2,0:T(8,128)S(1)} %convolution_add_fusion, f32[256,256]{0,1:T(8,128)S(1)} %copy.43, f32[256,256]{0,1:T(8,128)S(1)} %copy-done.2), kind=kOutput, calls=%fused_computation.21 | convolution fusion | flops 808910848 | bytes 11010048 | tf_op jit(solution)/shard_map/ka,gkb->gab/dot_general | solution.py:75
  155.4 4.0 %multiply_bitcast_fusion = f32[16,128,256]{1,2,0:T(8,128)} fusion(f32[16,256,128]{2,1,0:T(8,128)S(1)} %fusion.10, f32[16,256,256]{1,2,0:T(8,128)S(1)} %convolution_add_fusion, f32[16,256,256]{1,2,0:T(8,128)S(1)} %convolution_subtract_fusion, f32[256,256]{0,1:T(8,128)S(1)} %copy.43, f32[256,256]{0,1:T(8,128)S(1)} %copy-done.2), kind=kOutput, calls=%fused_computation.55 | convolution fusion | flops 809959424 | bytes 13107200 | tf_op jit(solution)/shard_map/ka,gkb->gab/dot_general | solution.py:75
  159.4 0.0 copy-start.6
  159.4 3.0 %copy.53 = f32[16,128,256]{2,1,0:T(8,128)} copy(f32[16,128,256]{1,2,0:T(8,128)} %multiply_bitcast_fusion) | data formatting | bytes 4194304 | tf_op jit(solution)/shard_map/div | solution.py:78
  162.4 2.9 %div.23 = f32[16,32,1024]{2,1,0:T(8,128)} reshape(f32[16,128,256]{2,1,0:T(8,128)} %copy.53) | data formatting | bytes 4194304 | tf_op jit(solution)/shard_map/div | solution.py:78
  165.3 0.0 copy-done.6
  165.3 0.0 copy-start.1
  165.3 2.4 %add_convert_fusion = bf16[16,32,1024]{2,1,0:T(8,128)(2,1)S(1)} fusion(f32[16,32,1024]{2,1,0:T(8,128)} %div.23, f32[16]{0:T(128)S(1)} %dynamic_slice.3, bf16[32,16,1024]{2,1,0:T(8,128)(2,1)S(1)} %copy-done.6), kind=kLoop, calls=%fused_computation.54 | loop fusion | flops 2097152 | bytes 4194368 | tf_op jit(solution)/shard_map/convert_element_type | solution.py:104
  167.7 0.6 copy.54
  168.3 24.1 %all_to_all.39 = bf16[16,32,1024]{2,0,1:T(8,128)(2,1)S(1)} all-to-all(bf16[16,32,1024]{2,0,1:T(8,128)(2,1)S(1)} %copy.54), channel_id=1, replica_groups=mesh['seq'=32,'ch'=8] {'seq'}, dimensions={1} | all-to-all | bytes 2097152 | tf_op jit(solution)/shard_map/all_to_all | solution.py:107
  192.4 2.9 %fusion.32 = bf16[512,1024]{1,0:T(8,128)(2,1)} fusion(f32[3,512,1024]{2,1,0:T(8,128)} %multiply_add_fusion, bf16[16,32,1024]{2,0,1:T(8,128)(2,1)S(1)} %all_to_all.39), kind=kLoop, calls=%fused_computation.53 | loop fusion | flops 1572864 | bytes 4194304 | tf_op jit(solution)/shard_map/convert_element_type | solution.py:108
  195.3 0.0 copy-done.1
  (6 shorter events, 0.1 us)
Async XLA Ops:
  0.0 28.7 %copy-start = (bf16[3,512,512]{2,1,0:T(8,128)(2,1)S(1)}, bf16[3,512,512]{2,1,0:T(8,128)(2,1)}, u32[]{:S(2)}) copy-start(bf16[3,512,512]{2,1,0:T(8,128)(2,1)} %param.8) | copy-start | bytes 4718596
  0.0 64.1 %all-to-all-start.1 = ((bf16[32,16,1024]{2,1,0:T(8,128)(2,1)}), bf16[32,16,1024]{2,1,0:T(8,128)(2,1)}, u32[]{:S(2)}, u32[]{:S(2)}) async-start(bf16[32,16,1024]{2,1,0:T(8,128)(2,1)} %bitcast.137), calls=%async_computation.1 | async-start | bytes 2097152 | tf_op jit(solution)/shard_map/all_to_all | solution.py:88
  33.1 10.2 %copy-start.7 = (f32[7,3,512]{2,0,1:T(8,128)S(1)}, f32[7,3,512]{2,0,1:T(8,128)}, u32[]{:S(2)}) copy-start(f32[7,3,512]{2,0,1:T(8,128)} %param.9) | copy-start | bytes 129028
  37.2 11.6 %collective-permute-start = (bf16[3,512,6]{2,1,0:T(8,128)(2,1)}, bf16[3,512,6]{2,1,0:T(8,128)(2,1)}, u32[]{:S(2)}, u32[]{:S(2)}) collective-permute-start(bf16[3,512,6]{2,1,0:T(8,128)(2,1)} %slice.68), channel_id=1, source_target_pairs={{0,8},{8,16},{16,24},{24,32},{32,40},{40,48},{48,56},{56,64},{64,7... | collective-permute-start | bytes 55304 | tf_op jit(solution)/shard_map/ppermute | solution.py:18
  64.2 42.2 %all-to-all-start = ((bf16[32,16,1024]{2,1,0:T(8,128)(2,1)}), bf16[32,16,1024]{2,1,0:T(8,128)(2,1)S(1)}, u32[]{:S(2)}, u32[]{:S(2)}) async-start(bf16[32,16,1024]{2,1,0:T(8,128)(2,1)} %bitcast.6), calls=%async_computation | async-start | bytes 2097152 | tf_op jit(solution)/shard_map/all_to_all | solution.py:101
  74.6 3.4 %copy-start.3 = (f32[256,256]{1,0:T(8,128)S(1)}, f32[256,256]{1,0:T(8,128)}, u32[]{:S(2)}) copy-start(f32[256,256]{1,0:T(8,128)} %get-tuple-element.20) | copy-start | bytes 786436
  74.6 3.4 %copy-start.4 = (f32[256,256]{1,0:T(8,128)S(1)}, f32[256,256]{1,0:T(8,128)}, u32[]{:S(2)}) copy-start(f32[256,256]{1,0:T(8,128)} %get-tuple-element.21) | copy-start | bytes 786436
  106.4 3.0 %copy-start.5 = (bf16[32,16,1024]{2,1,0:T(8,128)(2,1)}, bf16[32,16,1024]{2,1,0:T(8,128)(2,1)S(1)}, u32[]{:S(2)}) copy-start(bf16[32,16,1024]{2,1,0:T(8,128)(2,1)S(1)} %all-to-all-done) | copy-start | bytes 3145732
  107.6 3.5 %copy-start.2 = (f32[256,256]{0,1:T(8,128)S(1)}, f32[256,256]{0,1:T(8,128)}, u32[]{:S(2)}) copy-start(f32[256,256]{0,1:T(8,128)} %copy.41) | copy-start | bytes 786436
  159.4 5.9 %copy-start.6 = (bf16[32,16,1024]{2,1,0:T(8,128)(2,1)S(1)}, bf16[32,16,1024]{2,1,0:T(8,128)(2,1)}, u32[]{:S(2)}) copy-start(bf16[32,16,1024]{2,1,0:T(8,128)(2,1)} %copy-done.5) | copy-start | bytes 3145732
  165.3 30.1 %copy-start.1 = (bf16[3,512,512]{2,1,0:T(8,128)(2,1)S(1)}, bf16[3,512,512]{2,1,0:T(8,128)(2,1)}, u32[]{:S(2)}) copy-start(bf16[3,512,512]{2,1,0:T(8,128)(2,1)} %param.8) | copy-start | bytes 4718596
where the time goes:
time: 196 us
  matrix products  89 us (45%)
  blocking collectives  41.5 us (21%)
  other arithmetic  23.7 us (12%)
  starting transfers between devices  22.6 us (12%)
  local copies, waits for them, and re-layouts  18.3 us (9%)
    dot_general x12, matrix products, along_last(): return jnp.einsum('gkb,bm->gkm', left, table, precision=PRECISE)  69.6 us
    all_to_all x1, blocking collectives, shards(): lax.all_to_all(long_out, 'seq', split_axis=1, concat_axis=0, tiled=True)  24.1 us
    psum x1, blocking collectives, shards(): squares = lax.psum(jnp.sum(values * values, axis=0), 'ch')  17.4 us
    add x1, other arithmetic, short_conv(): acc_sum + weights[offset][:, :, None] * padded[:, :, begin:begin + filter...  11.8 us
    all_to_all x1, starting transfers between devices, shards(): lax.all_to_all(long_filter, 'seq', split_axis=0, concat_axis=1, tiled=True)  8.77 us
    all_to_all x1, starting transfers between devices, shards(): lax.all_to_all(gated_rows, 'seq', split_axis=0, concat_axis=1, tiled=True)  7.7 us
    ppermute x1, starting transfers between devices, passed_along(): return lax.ppermute(value, axis, pairs)  6.09 us
    div x2, local copies, waits for them, and re-layouts, long_conv(): return result.reshape(group_size, filter_extent) / fft_length  5.89 us
  transfers between devices with their start and end apart: 3, of which 0 were waited for; matrix products, arithmetic and copies ran while one was open for 34% of the time, Pallas kernels for 0%

commit v1 on v0

v1 whole, which is shorter than its diff:
```python
import jax
import jax.numpy as jnp
import numpy as np
from jax import lax
from jax.experimental import pallas as pl
from jax.experimental.pallas import tpu as pltpu
from jax.sharding import PartitionSpec as P

MIXER_CHANNELS = 4096
EPSILON = 1e-06

LANES = 128
OUTER = 256
TOKENS = OUTER * LANES
DEVICES = 32
EIGHTHS = 8
CHANNELS = 16
VOCAB = 512
TAPS = 7
PAD = 8
BATCH = 4
ID_SHIFT = 256
CONV = 4
UX = 4
UM = 16


def transform_tables():
    place = np.arange(OUTER)
    a = (place % DEVICES) * EIGHTHS + place // DEVICES
    k1 = np.arange(OUTER)
    b = np.arange(LANES)
    outer = 2 * np.pi * ((a[:, None] * (4 * k1[None, :] + 1)) % 1024) / 1024
    forward = np.concatenate([np.cos(outer), -np.sin(outer)], axis=1)
    backward = np.concatenate([np.cos(outer).T, -np.sin(outer).T], axis=0) / TOKENS
    twist = 2 * np.pi * (b[:, None] * (4 * k1[None, :] + 1)) / (4 * TOKENS)
    inner = 2 * np.pi * ((b[:, None] * b[None, :]) % LANES) / LANES
    cos, sin = np.cos(inner), np.sin(inner)
    inward = np.block([[cos, sin], [-sin, cos]])
    outward = np.block([[cos, -sin], [sin, cos]])
    half = lambda x: jnp.asarray(x.astype(np.float32)).astype(jnp.bfloat16)
    full = lambda x: jnp.asarray(x.astype(np.float32))
    return (
        half(forward),
        full(np.stack([np.cos(twist), np.sin(twist)])),
        half(inward),
        half(outward),
        half(backward),
    )


def pick_lanes(table, lanes):
    numbers = lax.GatherDimensionNumbers(
        offset_dims=(), collapsed_slice_dims=(1,), start_index_map=(1,),
        operand_batching_dims=(0,), start_indices_batching_dims=(0,),
    )
    return lax.gather(
        table, lanes[..., None], numbers, slice_sizes=(1, 1), mode=lax.GatherScatterMode.PROMISE_IN_BOUNDS
    )


def every(ref, first, count, step):
    return ref[pl.ds(first, count, stride=step), :]


def both_sides(ref, channel):
    return jnp.concatenate([every(ref.at[side], channel, LANES, CHANNELS) for side in range(2)], axis=1)


def mixer_kernel(
    skip_ref, mail_ref, table_ref, taps_ref, forward_hbm, twist_hbm, inward_hbm, outward_hbm, backward_hbm,
    out_ref,
    ids, ids_t, features, first, gated, taps, result, x_hat, h_hat,
    forward, twist, inward, outward, backward, sems,
):
    f32, bf16 = jnp.float32, jnp.bfloat16
    copies = [
        pltpu.make_async_copy(source, target, sems.at[i])
        for i, (source, target) in enumerate((
            (forward_hbm, forward), (twist_hbm, twist), (inward_hbm, inward),
            (outward_hbm, outward), (backward_hbm, backward),
        ))
    ]
    for copy in copies:
        copy.start()
    lane = lax.broadcasted_iota(jnp.int32, (CHANNELS, LANES), 1)

    for d in range(DEVICES):
        ids[d * EIGHTHS : (d + 1) * EIGHTHS] = mail_ref[d, :, 2 * EIGHTHS * LANES :].astype(f32)
    turned_ids = jnp.concatenate([every(ids, e, DEVICES, EIGHTHS) for e in range(EIGHTHS)], axis=0).T
    for side in range(2):
        ids_t[side] = turned_ids[:, side * LANES : (side + 1) * LANES].astype(jnp.int32) + ID_SHIFT

    def unpack(d, carry):
        for half in range(2):
            row = pl.multiple_of(d * CHANNELS + half * 8, 8)
            for e in range(EIGHTHS):
                column = (half * EIGHTHS + e) * LANES
                taps[e, pl.ds(row, 8), :] = mail_ref[d, :, column : column + LANES].astype(f32)
        return carry

    lax.fori_loop(0, DEVICES, unpack, 0, unroll=4)
    for copy in copies:
        copy.wait()

    def look_up(b):
        for side in range(2):
            token = jnp.broadcast_to(ids_t[side, pl.ds(b, 1), :], (CHANNELS, LANES))
            low = (token & (LANES - 1)).astype(jnp.int16)
            token = token.astype(jnp.int16)
            odd = (token & LANES) != 0
            upper = (token & (2 * LANES)) != 0
            for j in range(3):
                picks = [pick_lanes(table_ref[j, :, q * LANES : (q + 1) * LANES], low) for q in range(4)]
                features[j * 2 + side, b + PAD] = jnp.where(
                    upper, jnp.where(odd, picks[3], picks[2]), jnp.where(odd, picks[1], picks[0])
                )

    def transform(signals, store, start):
        z = jnp.dot(jnp.concatenate(signals, axis=0), forward[...], preferred_element_type=f32)
        cos, sin = twist[0], twist[1]
        for i in range(len(signals)):
            real, imag = z[i * LANES : (i + 1) * LANES, :OUTER], z[i * LANES : (i + 1) * LANES, OUTER:]
            turned = jnp.concatenate([real * cos + imag * sin, imag * cos - real * sin], axis=0)
            store[start + i] = jnp.dot(inward[...], turned.astype(bf16), preferred_element_type=f32).astype(
                store.dtype
            )

    def filters_of(start):
        transform(
            [
                jnp.concatenate(
                    [every(taps.at[e], start + i, DEVICES, CHANNELS) for e in range(EIGHTHS)], axis=0
                ).T.astype(bf16)
                for i in range(BATCH)
            ],
            h_hat, start,
        )

    def look_and_filter(block, carry):
        filters_of(block * BATCH)
        for i in range(LANES * BATCH // CHANNELS):
            look_up(block * (LANES * BATCH // CHANNELS) + i)
        return carry

    lax.fori_loop(0, CHANNELS // BATCH, look_and_filter, 0)

    for j in range(3):
        for back in range(1, TAPS):
            left = features[2 * j, PAD + LANES - back].astype(f32)
            right = features[2 * j + 1, PAD + LANES - back].astype(f32)
            by_32 = pltpu.roll(left, 32, 1)
            wrapped = jnp.where(lane == 0, 0.0, pltpu.roll(right, 33, 1))
            features[2 * j, PAD - back] = jnp.where(lane < 32, wrapped, by_32).astype(bf16)
            features[2 * j + 1, PAD - back] = jnp.where(lane < 32, by_32, pltpu.roll(right, 32, 1)).astype(bf16)

    def convolve(block, carry):
        start = block * CONV
        for side in range(2):
            sums = []
            for j in range(3):
                window = [
                    features[j * 2 + side, start + PAD - (TAPS - 1) + i].astype(f32)
                    for i in range(CONV + TAPS - 1)
                ]
                out = []
                for i in range(CONV):
                    total = taps_ref[j] * window[i + TAPS - 1]
                    for k in range(1, TAPS):
                        total = total + taps_ref[k * 3 + j] * window[i + TAPS - 1 - k]
                    out.append(total)
                sums.append(out)
            for i in range(CONV):
                row = pl.ds(pl.multiple_of((start + i) * CHANNELS, CHANNELS), CHANNELS)
                first[side, row, :] = sums[0][i]
                gated[side, row, :] = (sums[1][i] * sums[2][i]).astype(bf16).astype(f32)
        return carry

    lax.fori_loop(0, LANES // CONV, convolve, 0)

    def streams_of(block, carry):
        start = block * BATCH
        transform([both_sides(gated, start + i).astype(bf16) for i in range(BATCH)], x_hat, start)
        return carry

    lax.fori_loop(0, CHANNELS // BATCH, streams_of, 0, unroll=UX)

    def mix(c, carry):
        h_real, h_imag = h_hat[c, :LANES], h_hat[c, LANES:]
        x_real, x_imag = x_hat[c, :LANES].astype(f32), x_hat[c, LANES:].astype(f32)
        product = jnp.concatenate(
            [x_real * h_real - x_imag * h_imag, x_real * h_imag + x_imag * h_real], axis=0
        )
        p = jnp.dot(outward[...], product.astype(bf16), preferred_element_type=f32)
        real, imag = p[:LANES], p[LANES:]
        cos, sin = twist[0], twist[1]
        q = jnp.concatenate([real * cos - imag * sin, imag * cos + real * sin], axis=1)
        y = jnp.dot(q.astype(bf16), backward[...], preferred_element_type=f32)
        long_out = (y + skip_ref[c] * both_sides(gated, c)).astype(bf16).astype(f32)
        mixed = (both_sides(first, c) * long_out).T
        for e in range(EIGHTHS):
            result[e, pl.ds(c, DEVICES, stride=CHANNELS), :] = mixed[e * DEVICES : (e + 1) * DEVICES]
        return carry

    lax.fori_loop(0, CHANNELS, mix, 0, unroll=UM)
    for e in range(EIGHTHS):
        out_ref[:, e * LANES : (e + 1) * LANES] = result[e].astype(bf16)


def mix_tokens(skip, mail, table, taps):
    whole = pl.BlockSpec(memory_space=pltpu.VMEM)
    outside = pl.BlockSpec(memory_space=pl.ANY)
    bf16, f32 = jnp.bfloat16, jnp.float32
    tables = transform_tables()
    return pl.pallas_call(
        mixer_kernel,
        out_shape=jax.ShapeDtypeStruct((DEVICES * CHANNELS, EIGHTHS * LANES), bf16),
        in_specs=[pl.BlockSpec(memory_space=pltpu.SMEM), whole, whole, whole] + [outside] * len(tables),
        out_specs=whole,
        scratch_shapes=[
            pltpu.VMEM((OUTER, LANES), f32),
            pltpu.VMEM((2, LANES, LANES), jnp.int32),
            pltpu.VMEM((6, PAD + LANES, CHANNELS, LANES), bf16),
            pltpu.VMEM((2, LANES * CHANNELS, LANES), f32),
            pltpu.VMEM((2, LANES * CHANNELS, LANES), f32),
            pltpu.VMEM((EIGHTHS, DEVICES * CHANNELS, LANES), f32),
            pltpu.VMEM((EIGHTHS, DEVICES * CHANNELS, LANES), f32),
            pltpu.VMEM((CHANNELS, 2 * LANES, OUTER), bf16),
            pltpu.VMEM((CHANNELS, 2 * LANES, OUTER), f32),
        ]
        + [pltpu.VMEM(table.shape, table.dtype) for table in tables]
        + [pltpu.SemaphoreType.DMA((len(tables),))],
        compiler_params=pltpu.CompilerParams(vmem_limit_bytes=44 * 2**20),
        cost_estimate=pl.CostEstimate(flops=4 * 10**9, bytes_accessed=4 * 10**6, transcendentals=0),
        name="mixer",
    )(skip, mail, table, taps, *tables)


def ring_sum(value, axis):
    size = lax.axis_size(axis)
    assert size == 8

    def arriving_from(x, by):
        return lax.ppermute(x, axis, [((i + by) % size, i) for i in range(size)])

    after = arriving_from(value, 1)
    before = arriving_from(value, -1)
    pair = value + after
    three = pair + before
    return three + arriving_from(three, 3) + arriving_from(pair, -3)


def shards(token_ids, embedding, projected, short_taps, long_filter, skip_gain):
    rank = lax.axis_index("seq")

    filters = long_filter.reshape(DEVICES, 2, 8, EIGHTHS * LANES)
    ids = (token_ids - ID_SHIFT).astype(jnp.bfloat16).reshape(1, EIGHTHS, LANES)
    letters = jnp.concatenate(
        [filters[:, 0], filters[:, 1], jnp.broadcast_to(ids, (DEVICES, EIGHTHS, LANES))], axis=2
    )
    mail = lax.all_to_all(letters, "seq", split_axis=0, concat_axis=0, tiled=True)

    values = embedding.astype(jnp.float32)
    squares = ring_sum(jnp.sum(values * values, axis=0, keepdims=True), "ch")
    scale = 1.0 / jnp.sqrt(squares / MIXER_CHANNELS + EPSILON)
    own = lax.dynamic_slice_in_dim(projected, rank * CHANNELS, CHANNELS, axis=1)
    table = (own.astype(jnp.float32) * scale[None]).astype(jnp.bfloat16)

    own_taps = lax.dynamic_slice_in_dim(short_taps, rank * CHANNELS, CHANNELS, axis=2)
    taps = jnp.broadcast_to(own_taps.reshape(TAPS * 3, CHANNELS, 1), (TAPS * 3, CHANNELS, LANES))
    skip = lax.dynamic_slice_in_dim(skip_gain, rank * CHANNELS, CHANNELS)

    mixed = mix_tokens(skip, mail, table, taps)
    return lax.all_to_all(mixed, "seq", split_axis=0, concat_axis=0, tiled=True)


def solution(mesh):
    placed = (
        P("seq"),
        P("ch", None),
        P(None, "ch", None),
        P(None, None, "ch"),
        P("ch", "seq"),
        P("ch"),
    )
    return jax.shard_map(shards, mesh=mesh, in_specs=placed, out_specs=P("ch", "seq"), check_vma=False)
```

time: 196 us -> 72.9 us (0.37)
  matrix products: 89 us -> 0 us
  other arithmetic: 23.7 us -> 2.76 us
  Pallas kernels: 0 us -> 16.4 us
  blocking collectives: 41.5 us -> 25.5 us
  local copies, waits for them, and re-layouts: 18.3 us -> 3.22 us
  waiting for transfers between devices: 0.01 us -> 5.49 us
  starting transfers between devices: 22.6 us -> 19 us
    dot_general x20 -> x0, matrix products: 89 us -> none  [the longest x12 69.6 us: along_last(): return jnp.einsum('gkb,bm->gkm', left, table, precision=PRECISE)]
    psum x1 -> x0, blocking collectives: 17.4 us -> none  [shards(): squares = lax.psum(jnp.sum(values * values, axis=0), 'ch')]
    pallas_call x0 -> x1, Pallas kernels: none -> 16.4 us  [mix_tokens(): pl.pallas_call(mixer_kernel, out_shape=jax.ShapeDtypeStruct((DEVICES * CH...]
    add x1, other arithmetic: 11.8 us -> 0.01 us  [ring_sum(): three = pair + before]
    convert_element_type x3 -> x1, other arithmetic: 8.89 us -> 0.82 us  [shards(): table = (own.astype(jnp.float32) * scale[None]).astype(jnp.bfloat16)]
    all_to_all x2 -> x1, starting transfers between devices: 16.5 us -> 8.73 us  [shards(): lax.all_to_all(letters, 'seq', split_axis=0, concat_axis=0, tiled=True)]
    div x2 -> x0, local copies, waits for them, and re-layouts: 5.89 us -> none  [long_conv(): return result.reshape(group_size, filter_extent) / fft_length]
    ppermute x1 -> x4, waiting for transfers between devices: 0.01 us -> 4.59 us  [arriving_from(): return lax.ppermute(x, axis, [((i + by) % size, i) for i in range(size)])]
  transfers between devices with their start and end apart: 3 -> 5, of which waited for: 0 -> 4; matrix products, arithmetic and copies ran while one was open for 34% -> 3% of each run, Pallas kernels for 0% -> 0%
where the time goes in v1:
time: 72.9 us; the launch traced here: 72.5 us
  blocking collectives  25.5 us (35%)
  starting transfers between devices  19 us (26%)
  Pallas kernels  16.4 us (22%)
  waiting for transfers between devices  5.49 us (8%)
  local copies, waits for them, and re-layouts  3.22 us (4%)
  other arithmetic  2.76 us (4%)
    all_to_all x1, blocking collectives, shards(): return lax.all_to_all(mixed, 'seq', split_axis=0, concat_axis=0, tiled=True)  25.5 us
    pallas_call x1, Pallas kernels, mix_tokens(): pl.pallas_call(mixer_kernel, out_shape=jax.ShapeDtypeStruct((DEVICES * CH...  16.4 us
    ppermute x4, starting transfers between devices, arriving_from(): return lax.ppermute(x, axis, [((i + by) % size, i) for i in range(size)])  10.3 us
    all_to_all x1, starting transfers between devices, shards(): lax.all_to_all(letters, 'seq', split_axis=0, concat_axis=0, tiled=True)  8.73 us
    ppermute x4, waiting for transfers between devices, arriving_from(): return lax.ppermute(x, axis, [((i + by) % size, i) for i in range(size)])  4.59 us
  transfers between devices with their start and end apart: 5, of which 4 were waited for; matrix products, arithmetic and copies ran while one was open for 3% of the time, Pallas kernels for 0%

profile of v1, /device:TPU:1, one launch (start us, length us, event | category | flops | bytes accessed | tf_op | source)
XLA Modules:
  0.0 72.5 jit_solution(4455606786566683701)
XLA Ops:
  0.0 0.0 copy-start
  0.0 0.7 fusion
  0.7 1.3 %slice_bitcast_fusion.1 = (bf16[32,8,1024]{2,1,0:T(8,128)(2,1)S(1)}, bf16[32,8,1024]{2,1,0:T(8,128)(2,1)S(1)}) fusion(bf16[32,2,8,1024]{3,2,1,0:T(8,128)(2,1)} %bitcast.17), kind=kLoop, calls=%fused_computation.3 | loop fusion | bytes 2097152 | tf_op jit(solution)/shard_map/squeeze | solution.py:259
  2.0 1.1 %pad_maximum_fusion = bf16[32,8,2176]{2,1,0:T(8,128)(2,1)} fusion(bf16[32,8,128]{2,1,0:T(8,128)(2,1)S(1)} %broadcast_in_dim.19, bf16[32,8,1024]{2,1,0:T(8,128)(2,1)S(1)} %get-tuple-element.8, bf16[32,8,1024]{2,1,0:T(8,128)(2,1)S(1)} %get-tuple-element.7), kind=kLoop, calls=%fused_computation | loop fusion | flops 3342336 | bytes 2228224 | tf_op jit(solution)/shard_map/concatenate | solution.py:258
  3.1 0.0 copy-start.6
  3.1 0.0 copy-start.1
  3.1 0.0 copy-start.2
  3.1 0.0 copy-start.3
  3.1 0.0 copy-start.4
  3.1 0.0 copy-start.5
  3.1 8.7 %all-to-all-start = ((bf16[32,8,2176]{2,1,0:T(8,128)(2,1)}), bf16[32,8,2176]{2,1,0:T(8,128)(2,1)S(1)}, u32[]{:S(2)}, u32[]{:S(2)}) async-start(bf16[32,8,2176]{2,1,0:T(8,128)(2,1)} %pad_maximum_fusion), calls=%async_computation | async-start | bytes 2228224 | tf_op jit(solution)/shard_map/all_to_all | solution.py:261
  11.8 0.0 copy-done.6
  11.9 0.2 multiply_reduce_fusion
  12.0 1.7 %collective-permute-start.1 = (f32[1,512]{1,0:T(1,128)S(1)}, f32[1,512]{1,0:T(1,128)S(1)}, u32[]{:S(2)}, u32[]{:S(2)}) collective-permute-start(f32[1,512]{1,0:T(1,128)S(1)} %bitcast.18), channel_id=1, source_target_pairs={{7,0},{0,1},{1,2},{2,3},{3,4},{4,5},{5,6},{6,7},{15,8},{8,9},{9,10... | collective-permute-start | bytes 6152 | tf_op jit(solution)/shard_map/ppermute | solution.py:244
  13.7 4.0 %collective-permute-start = (f32[1,512]{1,0:T(1,128)S(1)}, f32[1,512]{1,0:T(1,128)S(1)}, u32[]{:S(2)}, u32[]{:S(2)}) collective-permute-start(f32[1,512]{1,0:T(1,128)S(1)} %bitcast.19), channel_id=1, source_target_pairs={{1,0},{2,1},{3,2},{4,3},{5,4},{6,5},{7,6},{0,7},{9,8},{10,9},{11,1... | collective-permute-start | bytes 6152 | tf_op jit(solution)/shard_map/ppermute | solution.py:244
  17.7 1.2 %collective-permute-done.1 = f32[1,512]{1,0:T(1,128)S(1)} collective-permute-done((f32[1,512]{1,0:T(1,128)S(1)}, f32[1,512]{1,0:T(1,128)S(1)}, u32[]{:S(2)}, u32[]{:S(2)}) %collective-permute-start.1) | collective-permute-done | bytes 2080 | tf_op jit(solution)/shard_map/ppermute | solution.py:244
  18.9 0.0 collective-permute-done
  18.9 4.3 %collective-permute-start.3 = (f32[1,512]{1,0:T(1,128)S(1)}, f32[1,512]{1,0:T(1,128)S(1)}, u32[]{:S(2)}, u32[]{:S(2)}) collective-permute-start(f32[1,512]{1,0:T(1,128)S(1)} %get-tuple-element.6), channel_id=1, source_target_pairs={{5,0},{6,1},{7,2},{0,3},{1,4},{2,5},{3,6},{4,7},{13,8},{14,9},{15,... | collective-permute-start | bytes 6152 | tf_op jit(solution)/shard_map/ppermute | solution.py:244
  23.2 0.3 collective-permute-start.2
  23.5 0.0 copy-done
  23.5 0.1 constant_dynamic-slice_fusion
  23.6 0.8 %dynamic_slice.9.skip_ref = f32[16]{0:T(128)S(1)} dynamic-slice(f32[512]{0:T(512)} %param.16, s32[]{:T(128)S(6)} %select_n.2), dynamic_slice_sizes={16} | dynamic-slice | bytes 132 | tf_op jit(solution)/shard_map/dynamic_slice | solution.py:271
  24.3 0.4 collective-permute-done.3
  24.8 3.0 %collective-permute-done.2 = f32[1,512]{1,0:T(1,128)S(1)} collective-permute-done((f32[1,512]{1,0:T(1,128)S(1)}, f32[1,512]{1,0:T(1,128)S(1)}, u32[]{:S(2)}, u32[]{:S(2)}) %collective-permute-start.2) | collective-permute-done | bytes 2080 | tf_op jit(solution)/shard_map/ppermute | solution.py:244
  27.8 0.8 %multiply_convert_fusion.table_ref = bf16[3,16,512]{2,1,0:T(8,128)(2,1)S(1)} fusion(f32[512]{0:T(512)S(1)} %bitcast.21, bf16[3,512,512]{2,1,0:T(8,128)(2,1)} %param.13, s32[]{:T(128)S(6)} %select_n.2), kind=kLoop, calls=%fused_computation.4 | loop fusion | flops 73728 | bytes 100356 | tf_op jit(solution)/shard_map/convert_element_type | solution.py:267
  28.6 0.9 %all-to-all-done.mail_ref = bf16[32,8,2176]{2,1,0:T(8,128)(2,1)S(1)} async-done(((bf16[32,8,2176]{2,1,0:T(8,128)(2,1)}), bf16[32,8,2176]{2,1,0:T(8,128)(2,1)S(1)}, u32[]{:S(2)}, u32[]{:S(2)}) %all-to-all-start) | async-done | bytes 1114144 | tf_op jit(solution)/shard_map/all_to_all | solution.py:261
  29.5 0.1 broadcast_in_dim.22.taps_ref
  29.6 0.0 copy-done.1
  29.6 0.0 copy-done.2
  29.6 0.0 copy-done.3
  29.6 0.0 copy-done.4
  29.6 0.0 copy-done.5
  29.6 16.4 %mixer.1 = bf16[512,1024]{1,0:T(8,128)(2,1)S(1)} custom-call(f32[16]{0:T(128)S(1)} %dynamic_slice.9.skip_ref, bf16[32,8,2176]{2,1,0:T(8,128)(2,1)S(1)} %all-to-all-done.mail_ref, bf16[3,16,512]{2,1,0:T(8,128)(2,1)S(1)} %multiply_convert_fusion.table_ref, f32[21,16,128]{2,1,0:T(8,128)S(1)} %broadcast_in_dim.22.taps_ref, bf16[256,512]{1,0:T(8,128)(2,1)S(1)} %copy-done.1, ...), custom_call_target="tpu_custom_call" | custom-call | flops 4000000000 | bytes 4000000 | tf_op jit(solution)/shard_map/mixer/pallas_call | solution.py:215
  46.1 25.5 %all_to_all.17 = bf16[32,16,1024]{2,1,0:T(8,128)(2,1)S(1)} all-to-all(bf16[32,16,1024]{2,1,0:T(8,128)(2,1)S(1)} %bitcast.15), channel_id=1, replica_groups=mesh['seq'=32,'ch'=8] {'seq'}, dimensions={0} | all-to-all | bytes 2097152 | tf_op jit(solution)/shard_map/all_to_all | solution.py:274
  71.6 1.0 %copy.18 = bf16[512,1024]{1,0:T(8,128)(2,1)} copy(bf16[512,1024]{1,0:T(8,128)(2,1)S(1)} %bitcast.16) | data formatting | bytes 2097152
  (5 shorter events, 0.0 us)
Async XLA Ops:
  0.0 23.5 %copy-start = (f32[7,3,512]{2,0,1:T(8,128)S(1)}, f32[7,3,512]{2,0,1:T(8,128)}, u32[]{:S(2)}) copy-start(f32[7,3,512]{2,0,1:T(8,128)} %param.14) | copy-start | bytes 129028
  3.1 8.8 %copy-start.6 = (bf16[512,512]{1,0:T(8,128)(2,1)S(1)}, bf16[512,512]{1,0:T(8,128)(2,1)}, u32[]{:S(2)}) copy-start(bf16[512,512]{1,0:T(8,128)(2,1)} %param.12) | copy-start | bytes 1572868
  3.1 26.5 %copy-start.1 = (bf16[256,512]{1,0:T(8,128)(2,1)S(1)}, bf16[256,512]{1,0:T(8,128)(2,1)}, u32[]{:S(2)}) copy-start(bf16[256,512]{1,0:T(8,128)(2,1)} %constant.38.forward_hbm) | copy-start | bytes 786436
  3.1 26.5 %copy-start.2 = (f32[2,128,256]{2,1,0:T(8,128)S(1)}, f32[2,128,256]{2,1,0:T(8,128)}, u32[]{:S(2)}) copy-start(f32[2,128,256]{2,1,0:T(8,128)} %constant.34.clone.twist_hbm) | copy-start | bytes 786436
  3.1 26.5 %copy-start.3 = (bf16[512,256]{1,0:T(8,128)(2,1)S(1)}, bf16[512,256]{1,0:T(8,128)(2,1)}, u32[]{:S(2)}) copy-start(bf16[512,256]{1,0:T(8,128)(2,1)} %constant.41.backward_hbm) | copy-start | bytes 786436
  3.1 26.5 %copy-start.4 = (bf16[256,256]{1,0:T(8,128)(2,1)S(1)}, bf16[256,256]{1,0:T(8,128)(2,1)}, u32[]{:S(2)}) copy-start(bf16[256,256]{1,0:T(8,128)(2,1)} %constant.39.inward_hbm) | copy-start | bytes 393220
  3.1 26.5 %copy-start.5 = (bf16[256,256]{1,0:T(8,128)(2,1)S(1)}, bf16[256,256]{1,0:T(8,128)(2,1)}, u32[]{:S(2)}) copy-start(bf16[256,256]{1,0:T(8,128)(2,1)} %constant.40.outward_hbm) | copy-start | bytes 393220
  3.1 26.4 %all-to-all-start = ((bf16[32,8,2176]{2,1,0:T(8,128)(2,1)}), bf16[32,8,2176]{2,1,0:T(8,128)(2,1)S(1)}, u32[]{:S(2)}, u32[]{:S(2)}) async-start(bf16[32,8,2176]{2,1,0:T(8,128)(2,1)} %pad_maximum_fusion), calls=%async_computation | async-start | bytes 2228224 | tf_op jit(solution)/shard_map/all_to_all | solution.py:261
  12.0 6.9 %collective-permute-start.1 = (f32[1,512]{1,0:T(1,128)S(1)}, f32[1,512]{1,0:T(1,128)S(1)}, u32[]{:S(2)}, u32[]{:S(2)}) collective-permute-start(f32[1,512]{1,0:T(1,128)S(1)} %bitcast.18), channel_id=1, source_target_pairs={{7,0},{0,1},{1,2},{2,3},{3,4},{4,5},{5,6},{6,7},{15,8},{8,9},{9,10... | collective-permute-start | bytes 6152 | tf_op jit(solution)/shard_map/ppermute | solution.py:244
  13.7 5.2 %collective-permute-start = (f32[1,512]{1,0:T(1,128)S(1)}, f32[1,512]{1,0:T(1,128)S(1)}, u32[]{:S(2)}, u32[]{:S(2)}) collective-permute-start(f32[1,512]{1,0:T(1,128)S(1)} %bitcast.19), channel_id=1, source_target_pairs={{1,0},{2,1},{3,2},{4,3},{5,4},{6,5},{7,6},{0,7},{9,8},{10,9},{11,1... | collective-permute-start | bytes 6152 | tf_op jit(solution)/shard_map/ppermute | solution.py:244
  18.9 5.8 %collective-permute-start.3 = (f32[1,512]{1,0:T(1,128)S(1)}, f32[1,512]{1,0:T(1,128)S(1)}, u32[]{:S(2)}, u32[]{:S(2)}) collective-permute-start(f32[1,512]{1,0:T(1,128)S(1)} %get-tuple-element.6), channel_id=1, source_target_pairs={{5,0},{6,1},{7,2},{0,3},{1,4},{2,5},{3,6},{4,7},{13,8},{14,9},{15,... | collective-permute-start | bytes 6152 | tf_op jit(solution)/shard_map/ppermute | solution.py:244
  23.2 4.5 %collective-permute-start.2 = (f32[1,512]{1,0:T(1,128)S(1)}, f32[1,512]{1,0:T(1,128)S(1)}, u32[]{:S(2)}, u32[]{:S(2)}) collective-permute-start(f32[1,512]{1,0:T(1,128)S(1)} %get-tuple-element.5), channel_id=1, source_target_pairs={{3,0},{4,1},{5,2},{6,3},{7,4},{0,5},{1,6},{2,7},{11,8},{12,9},{13,... | collective-permute-start | bytes 6152 | tf_op jit(solution)/shard_map/ppermute | solution.py:244

commit v2 on v1

--- a/solution.py
+++ b/solution.py
@@ -20,9 +20,9 @@
 PAD = 8
 BATCH = 4
 ID_SHIFT = 256
+STEP = 8
 CONV = 4
-UX = 4
-UM = 16
+SHARE = 16
 
 
 def transform_tables():
@@ -70,7 +70,7 @@
 def mixer_kernel(
     skip_ref, mail_ref, table_ref, taps_ref, forward_hbm, twist_hbm, inward_hbm, outward_hbm, backward_hbm,
     out_ref,
-    ids, ids_t, features, first, gated, taps, result, x_hat, h_hat,
+    ids, ids_t, features, first, gated, taps, result, h_hat,
     forward, twist, inward, outward, backward, sems,
 ):
     f32, bf16 = jnp.float32, jnp.bfloat16
@@ -100,9 +100,6 @@
         return carry
 
     lax.fori_loop(0, DEVICES, unpack, 0, unroll=4)
-    for copy in copies:
-        copy.wait()
-
     def look_up(b):
         for side in range(2):
             token = jnp.broadcast_to(ids_t[side, pl.ds(b, 1), :], (CHANNELS, LANES))
@@ -114,54 +111,44 @@
                 picks = [pick_lanes(table_ref[j, :, q * LANES : (q + 1) * LANES], low) for q in range(4)]
                 features[j * 2 + side, b + PAD] = jnp.where(
                     upper, jnp.where(odd, picks[3], picks[2]), jnp.where(odd, picks[1], picks[0])
-                )
-
-    def transform(signals, store, start):
+                ).astype(f32)
+
+    def transform(signals):
         z = jnp.dot(jnp.concatenate(signals, axis=0), forward[...], preferred_element_type=f32)
         cos, sin = twist[0], twist[1]
+        out = []
         for i in range(len(signals)):
             real, imag = z[i * LANES : (i + 1) * LANES, :OUTER], z[i * LANES : (i + 1) * LANES, OUTER:]
             turned = jnp.concatenate([real * cos + imag * sin, imag * cos - real * sin], axis=0)
-            store[start + i] = jnp.dot(inward[...], turned.astype(bf16), preferred_element_type=f32).astype(
-                store.dtype
-            )
-
-    def filters_of(start):
-        transform(
-            [
-                jnp.concatenate(
-                    [every(taps.at[e], start + i, DEVICES, CHANNELS) for e in range(EIGHTHS)], axis=0
-                ).T.astype(bf16)
-                for i in range(BATCH)
-            ],
-            h_hat, start,
-        )
-
-    def look_and_filter(block, carry):
-        filters_of(block * BATCH)
-        for i in range(LANES * BATCH // CHANNELS):
-            look_up(block * (LANES * BATCH // CHANNELS) + i)
-        return carry
-
-    lax.fori_loop(0, CHANNELS // BATCH, look_and_filter, 0)
-
-    for j in range(3):
-        for back in range(1, TAPS):
-            left = features[2 * j, PAD + LANES - back].astype(f32)
-            right = features[2 * j + 1, PAD + LANES - back].astype(f32)
-            by_32 = pltpu.roll(left, 32, 1)
-            wrapped = jnp.where(lane == 0, 0.0, pltpu.roll(right, 33, 1))
-            features[2 * j, PAD - back] = jnp.where(lane < 32, wrapped, by_32).astype(bf16)
-            features[2 * j + 1, PAD - back] = jnp.where(lane < 32, by_32, pltpu.roll(right, 32, 1)).astype(bf16)
-
-    def convolve(block, carry):
-        start = block * CONV
+            out.append(jnp.dot(inward[...], turned.astype(bf16), preferred_element_type=f32))
+        return out
+
+    def transform_filters(start, count):
+        found = transform([
+            jnp.concatenate([every(taps.at[e], start + i, DEVICES, CHANNELS) for e in range(EIGHTHS)], axis=0)
+            .T.astype(bf16)
+            for i in range(count)
+        ])
+        for i, value in enumerate(found):
+            h_hat[start + i, :LANES] = value[:LANES] + skip_ref[start + i]
+            h_hat[start + i, LANES:] = value[LANES:]
+
+    def carry_over():
+        for j in range(3):
+            for back in range(1, TAPS):
+                left = features[2 * j, PAD + LANES - back]
+                right = features[2 * j + 1, PAD + LANES - back]
+                by_32 = pltpu.roll(left, 32, 1)
+                wrapped = jnp.where(lane == 0, 0.0, pltpu.roll(right, 33, 1))
+                features[2 * j, PAD - back] = jnp.where(lane < 32, wrapped, by_32)
+                features[2 * j + 1, PAD - back] = jnp.where(lane < 32, by_32, pltpu.roll(right, 32, 1))
+
+    def convolve(start):
         for side in range(2):
             sums = []
             for j in range(3):
                 window = [
-                    features[j * 2 + side, start + PAD - (TAPS - 1) + i].astype(f32)
-                    for i in range(CONV + TAPS - 1)
+                    features[j * 2 + side, start + PAD - (TAPS - 1) + i] for i in range(CONV + TAPS - 1)
                 ]
                 out = []
                 for i in range(CONV):
@@ -171,38 +158,47 @@
                     out.append(total)
                 sums.append(out)
             for i in range(CONV):
-                row = pl.ds(pl.multiple_of((start + i) * CHANNELS, CHANNELS), CHANNELS)
+                row = pl.ds((start + i) * CHANNELS, CHANNELS)
                 first[side, row, :] = sums[0][i]
                 gated[side, row, :] = (sums[1][i] * sums[2][i]).astype(bf16).astype(f32)
-        return carry
-
-    lax.fori_loop(0, LANES // CONV, convolve, 0)
-
-    def streams_of(block, carry):
-        start = block * BATCH
-        transform([both_sides(gated, start + i).astype(bf16) for i in range(BATCH)], x_hat, start)
-        return carry
-
-    lax.fori_loop(0, CHANNELS // BATCH, streams_of, 0, unroll=UX)
-
-    def mix(c, carry):
-        h_real, h_imag = h_hat[c, :LANES], h_hat[c, LANES:]
-        x_real, x_imag = x_hat[c, :LANES].astype(f32), x_hat[c, LANES:].astype(f32)
-        product = jnp.concatenate(
-            [x_real * h_real - x_imag * h_imag, x_real * h_imag + x_imag * h_real], axis=0
-        )
-        p = jnp.dot(outward[...], product.astype(bf16), preferred_element_type=f32)
-        real, imag = p[:LANES], p[LANES:]
-        cos, sin = twist[0], twist[1]
-        q = jnp.concatenate([real * cos - imag * sin, imag * cos + real * sin], axis=1)
-        y = jnp.dot(q.astype(bf16), backward[...], preferred_element_type=f32)
-        long_out = (y + skip_ref[c] * both_sides(gated, c)).astype(bf16).astype(f32)
-        mixed = (both_sides(first, c) * long_out).T
-        for e in range(EIGHTHS):
-            result[e, pl.ds(c, DEVICES, stride=CHANNELS), :] = mixed[e * DEVICES : (e + 1) * DEVICES]
-        return carry
-
-    lax.fori_loop(0, CHANNELS, mix, 0, unroll=UM)
+
+    steps = LANES // STEP
+    for i in range(STEP):
+        look_up(LANES - STEP + i)
+    carry_over()
+    for i in range(STEP):
+        look_up(i)
+    for copy in copies:
+        copy.wait()
+    for block in range(steps):
+        if block + 1 < steps - 1:
+            for i in range(STEP):
+                look_up((block + 1) * STEP + i)
+        transform_filters(block * CHANNELS // steps, CHANNELS // steps)
+        for i in range(0, STEP, CONV):
+            convolve(block * STEP + i)
+
+    for start in range(0, CHANNELS, BATCH):
+        streams = transform([both_sides(gated, start + i).astype(bf16) for i in range(BATCH)])
+        turned = []
+        for i in range(BATCH):
+            h_real, h_imag = h_hat[start + i, :LANES], h_hat[start + i, LANES:]
+            x_real, x_imag = streams[i][:LANES], streams[i][LANES:]
+            product = jnp.concatenate(
+                [x_real * h_real - x_imag * h_imag, x_real * h_imag + x_imag * h_real], axis=0
+            )
+            p = jnp.dot(outward[...], product.astype(bf16), preferred_element_type=f32)
+            real, imag = p[:LANES], p[LANES:]
+            cos, sin = twist[0], twist[1]
+            turned.append(
+                jnp.concatenate([real * cos - imag * sin, imag * cos + real * sin], axis=1).astype(bf16)
+            )
+        long_out = jnp.dot(jnp.concatenate(turned, axis=0), backward[...], preferred_element_type=f32)
+        for i in range(BATCH):
+            rounded = long_out[i * LANES : (i + 1) * LANES].astype(bf16).astype(f32)
+            mixed = (both_sides(first, start + i) * rounded).T
+            for e in range(EIGHTHS):
+                result[e, pl.ds(start + i, DEVICES, stride=CHANNELS), :] = mixed[e * DEVICES : (e + 1) * DEVICES]
     for e in range(EIGHTHS):
         out_ref[:, e * LANES : (e + 1) * LANES] = result[e].astype(bf16)
 
@@ -220,12 +216,11 @@
         scratch_shapes=[
             pltpu.VMEM((OUTER, LANES), f32),
             pltpu.VMEM((2, LANES, LANES), jnp.int32),
-            pltpu.VMEM((6, PAD + LANES, CHANNELS, LANES), bf16),
+            pltpu.VMEM((6, PAD + LANES, CHANNELS, LANES), f32),
             pltpu.VMEM((2, LANES * CHANNELS, LANES), f32),
             pltpu.VMEM((2, LANES * CHANNELS, LANES), f32),
             pltpu.VMEM((EIGHTHS, DEVICES * CHANNELS, LANES), f32),
             pltpu.VMEM((EIGHTHS, DEVICES * CHANNELS, LANES), f32),
-            pltpu.VMEM((CHANNELS, 2 * LANES, OUTER), bf16),
             pltpu.VMEM((CHANNELS, 2 * LANES, OUTER), f32),
         ]
         + [pltpu.VMEM(table.shape, table.dtype) for table in tables]
@@ -236,6 +231,30 @@
     )(skip, mail, table, taps, *tables)
 
 
+def letters_kernel(filter_ref, ids_ref, out_ref):
+    width = EIGHTHS * LANES
+    for half in range(2):
+        out_ref[:, :, half * width : (half + 1) * width] = filter_ref[:, half]
+    ids = (ids_ref[...] - ID_SHIFT).astype(jnp.float32).astype(jnp.bfloat16)
+    out_ref[:, :, 2 * width :] = jnp.broadcast_to(ids[None], (out_ref.shape[0], EIGHTHS, LANES))
+
+
+def write_letters(filters, ids):
+    width = EIGHTHS * LANES
+    return pl.pallas_call(
+        letters_kernel,
+        out_shape=jax.ShapeDtypeStruct((DEVICES, 8, 2 * width + LANES), jnp.bfloat16),
+        grid=(DEVICES // SHARE,),
+        in_specs=[
+            pl.BlockSpec((SHARE, 2, 8, width), lambda i: (i, 0, 0, 0)),
+            pl.BlockSpec((EIGHTHS, LANES), lambda i: (0, 0)),
+        ],
+        out_specs=pl.BlockSpec((SHARE, 8, 2 * width + LANES), lambda i: (i, 0, 0)),
+        cost_estimate=pl.CostEstimate(flops=0, bytes_accessed=2 * 2**20, transcendentals=0),
+        name="letters",
+    )(filters, ids)
+
+
 def ring_sum(value, axis):
     size = lax.axis_size(axis)
     assert size == 8
@@ -253,15 +272,14 @@
 def shards(token_ids, embedding, projected, short_taps, long_filter, skip_gain):
     rank = lax.axis_index("seq")
 
-    filters = long_filter.reshape(DEVICES, 2, 8, EIGHTHS * LANES)
-    ids = (token_ids - ID_SHIFT).astype(jnp.bfloat16).reshape(1, EIGHTHS, LANES)
-    letters = jnp.concatenate(
-        [filters[:, 0], filters[:, 1], jnp.broadcast_to(ids, (DEVICES, EIGHTHS, LANES))], axis=2
+    values = embedding.astype(jnp.float32)
+    partial = jnp.sum(values * values, axis=0, keepdims=True)
+    squares = ring_sum(partial, "ch")
+    letters = write_letters(
+        long_filter.reshape(DEVICES, 2, 8, EIGHTHS * LANES), token_ids.reshape(EIGHTHS, LANES)
     )
     mail = lax.all_to_all(letters, "seq", split_axis=0, concat_axis=0, tiled=True)
 
-    values = embedding.astype(jnp.float32)
-    squares = ring_sum(jnp.sum(values * values, axis=0, keepdims=True), "ch")
     scale = 1.0 / jnp.sqrt(squares / MIXER_CHANNELS + EPSILON)
     own = lax.dynamic_slice_in_dim(projected, rank * CHANNELS, CHANNELS, axis=1)
     table = (own.astype(jnp.float32) * scale[None]).astype(jnp.bfloat16)

time: 72.9 us -> 68.9 us (0.945)
  other arithmetic: 2.76 us -> 0.99 us
  local copies, waits for them, and re-layouts: 3.22 us -> 1.95 us
  Pallas kernels: 16.4 us -> 15.5 us
    pallas_call x1, Pallas kernels: 16.4 us -> 13.4 us  [mix_tokens(): pl.pallas_call(mixer_kernel, out_shape=jax.ShapeDtypeStruct((DEVICES * CH...]
    pallas_call x0 -> x1, Pallas kernels: none -> 2.1 us  [write_letters(): pl.pallas_call(letters_kernel, out_shape=jax.ShapeDtypeStruct((DEVICES, 8...]
    squeeze x1 -> x0, local copies, waits for them, and re-layouts: 1.27 us -> none  [shards(): filters[:, 0]]
    concatenate x1 -> x0, other arithmetic: 1.07 us -> none  [shards(): jnp.concatenate([filters[:, 0], filters[:, 1], jnp.broadcast_to(ids, (DEV...]
where the time goes in v2:
time: 68.9 us; the launch traced here: 68.6 us
  blocking collectives  25.5 us (37%)
  starting transfers between devices  19 us (28%)
  Pallas kernels  15.5 us (22%)
  waiting for transfers between devices  5.49 us (8%)
  local copies, waits for them, and re-layouts  1.95 us (3%)
  other arithmetic  0.99 us (1%)
    all_to_all x1, blocking collectives, shards(): return lax.all_to_all(mixed, 'seq', split_axis=0, concat_axis=0, tiled=True)  25.5 us
    pallas_call x1, Pallas kernels, mix_tokens(): pl.pallas_call(mixer_kernel, out_shape=jax.ShapeDtypeStruct((DEVICES * CH...  13.4 us
    ppermute x4, starting transfers between devices, arriving_from(): return lax.ppermute(x, axis, [((i + by) % size, i) for i in range(size)])  10.3 us
    all_to_all x1, starting transfers between devices, shards(): lax.all_to_all(letters, 'seq', split_axis=0, concat_axis=0, tiled=True)  8.73 us
    ppermute x4, waiting for transfers between devices, arriving_from(): return lax.ppermute(x, axis, [((i + by) % size, i) for i in range(size)])  4.59 us
    pallas_call x1, Pallas kernels, write_letters(): pl.pallas_call(letters_kernel, out_shape=jax.ShapeDtypeStruct((DEVICES, 8...  2.1 us
  transfers between devices with their start and end apart: 5, of which 4 were waited for; matrix products, arithmetic and copies ran while one was open for 3% of the time, Pallas kernels for 0%

profile of v2, /device:TPU:1, one launch (start us, length us, event | category | flops | bytes accessed | tf_op | source)
XLA Modules:
  0.0 68.6 jit_solution(9581669204718860953)
XLA Ops:
  0.0 0.0 copy-start
  0.0 2.1 %letters.1 = bf16[32,8,2176]{2,1,0:T(8,128)(2,1)} custom-call(bf16[32,2,8,1024]{3,2,1,0:T(8,128)(2,1)} %bitcast.8, s32[8,128]{1,0:T(8,128)} %bitcast.13), custom_call_target="tpu_custom_call" | custom-call | bytes 2097152 | tf_op jit(solution)/shard_map/letters/pallas_call | solution.py:244
  2.1 0.0 copy-start.6
  2.1 0.0 copy-start.1
  2.1 0.0 copy-start.2
  2.1 0.0 copy-start.3
  2.1 0.0 copy-start.4
  2.1 0.0 copy-start.5
  2.2 8.7 %all-to-all-start = ((bf16[32,8,2176]{2,1,0:T(8,128)(2,1)}), bf16[32,8,2176]{2,1,0:T(8,128)(2,1)S(1)}, u32[]{:S(2)}, u32[]{:S(2)}) async-start(bf16[32,8,2176]{2,1,0:T(8,128)(2,1)} %letters.1), calls=%async_computation | async-start | bytes 2228224 | tf_op jit(solution)/shard_map/all_to_all | solution.py:281
  10.9 0.0 copy-done.6
  10.9 0.2 multiply_reduce_fusion
  11.1 1.7 %collective-permute-start.1 = (f32[1,512]{1,0:T(1,128)S(1)}, f32[1,512]{1,0:T(1,128)S(1)}, u32[]{:S(2)}, u32[]{:S(2)}) collective-permute-start(f32[1,512]{1,0:T(1,128)S(1)} %bitcast.9), channel_id=1, source_target_pairs={{7,0},{0,1},{1,2},{2,3},{3,4},{4,5},{5,6},{6,7},{15,8},{8,9},{9,10... | collective-permute-start | bytes 6152 | tf_op jit(solution)/shard_map/ppermute | solution.py:263
  12.8 4.0 %collective-permute-start = (f32[1,512]{1,0:T(1,128)S(1)}, f32[1,512]{1,0:T(1,128)S(1)}, u32[]{:S(2)}, u32[]{:S(2)}) collective-permute-start(f32[1,512]{1,0:T(1,128)S(1)} %bitcast.10), channel_id=1, source_target_pairs={{1,0},{2,1},{3,2},{4,3},{5,4},{6,5},{7,6},{0,7},{9,8},{10,9},{11,1... | collective-permute-start | bytes 6152 | tf_op jit(solution)/shard_map/ppermute | solution.py:263
  16.8 1.2 %collective-permute-done.1 = f32[1,512]{1,0:T(1,128)S(1)} collective-permute-done((f32[1,512]{1,0:T(1,128)S(1)}, f32[1,512]{1,0:T(1,128)S(1)}, u32[]{:S(2)}, u32[]{:S(2)}) %collective-permute-start.1) | collective-permute-done | bytes 2080 | tf_op jit(solution)/shard_map/ppermute | solution.py:263
  18.0 0.0 collective-permute-done
  18.0 4.3 %collective-permute-start.3 = (f32[1,512]{1,0:T(1,128)S(1)}, f32[1,512]{1,0:T(1,128)S(1)}, u32[]{:S(2)}, u32[]{:S(2)}) collective-permute-start(f32[1,512]{1,0:T(1,128)S(1)} %get-tuple-element.6), channel_id=1, source_target_pairs={{5,0},{6,1},{7,2},{0,3},{1,4},{2,5},{3,6},{4,7},{13,8},{14,9},{15,... | collective-permute-start | bytes 6152 | tf_op jit(solution)/shard_map/ppermute | solution.py:263
  22.3 0.3 collective-permute-start.2
  22.5 0.0 copy-done
  22.5 0.1 constant_dynamic-slice_fusion
  22.6 0.8 %dynamic_slice.9.skip_ref = f32[16]{0:T(128)S(1)} dynamic-slice(f32[512]{0:T(512)} %param.16, s32[]{:T(128)S(6)} %select_n.2), dynamic_slice_sizes={16} | dynamic-slice | bytes 132 | tf_op jit(solution)/shard_map/dynamic_slice | solution.py:289
  23.4 0.4 collective-permute-done.3
  23.8 3.0 %collective-permute-done.2 = f32[1,512]{1,0:T(1,128)S(1)} collective-permute-done((f32[1,512]{1,0:T(1,128)S(1)}, f32[1,512]{1,0:T(1,128)S(1)}, u32[]{:S(2)}, u32[]{:S(2)}) %collective-permute-start.2) | collective-permute-done | bytes 2080 | tf_op jit(solution)/shard_map/ppermute | solution.py:263
  26.8 0.8 %multiply_convert_fusion.table_ref = bf16[3,16,512]{2,1,0:T(8,128)(2,1)S(1)} fusion(f32[512]{0:T(512)S(1)} %bitcast.12, bf16[3,512,512]{2,1,0:T(8,128)(2,1)} %param.13, s32[]{:T(128)S(6)} %select_n.2), kind=kLoop, calls=%fused_computation.1 | loop fusion | flops 73728 | bytes 100356 | tf_op jit(solution)/shard_map/convert_element_type | solution.py:285
  27.6 0.9 %all-to-all-done.mail_ref = bf16[32,8,2176]{2,1,0:T(8,128)(2,1)S(1)} async-done(((bf16[32,8,2176]{2,1,0:T(8,128)(2,1)}), bf16[32,8,2176]{2,1,0:T(8,128)(2,1)S(1)}, u32[]{:S(2)}, u32[]{:S(2)}) %all-to-all-start) | async-done | bytes 1114144 | tf_op jit(solution)/shard_map/all_to_all | solution.py:281
  28.5 0.1 broadcast_in_dim.13.taps_ref
  28.6 0.0 copy-done.1
  28.7 0.0 copy-done.2
  28.7 0.0 copy-done.3
  28.7 0.0 copy-done.4
  28.7 0.0 copy-done.5
  28.7 13.4 %mixer.1 = bf16[512,1024]{1,0:T(8,128)(2,1)S(1)} custom-call(f32[16]{0:T(128)S(1)} %dynamic_slice.9.skip_ref, bf16[32,8,2176]{2,1,0:T(8,128)(2,1)S(1)} %all-to-all-done.mail_ref, bf16[3,16,512]{2,1,0:T(8,128)(2,1)S(1)} %multiply_convert_fusion.table_ref, f32[21,16,128]{2,1,0:T(8,128)S(1)} %broadcast_in_dim.13.taps_ref, bf16[256,512]{1,0:T(8,128)(2,1)S(1)} %copy-done.1, ...), custom_call_target="tpu_custom_call" | custom-call | flops 4000000000 | bytes 4000000 | tf_op jit(solution)/shard_map/mixer/pallas_call | solution.py:211
  42.1 25.5 %all_to_all.17 = bf16[32,16,1024]{2,1,0:T(8,128)(2,1)S(1)} all-to-all(bf16[32,16,1024]{2,1,0:T(8,128)(2,1)S(1)} %bitcast.6), channel_id=1, replica_groups=mesh['seq'=32,'ch'=8] {'seq'}, dimensions={0} | all-to-all | bytes 2097152 | tf_op jit(solution)/shard_map/all_to_all | solution.py:292
  67.6 1.0 %copy.14 = bf16[512,1024]{1,0:T(8,128)(2,1)} copy(bf16[512,1024]{1,0:T(8,128)(2,1)S(1)} %bitcast.7) | data formatting | bytes 2097152
  (4 shorter events, 0.0 us)
Async XLA Ops:
  0.0 22.5 %copy-start = (f32[7,3,512]{2,0,1:T(8,128)S(1)}, f32[7,3,512]{2,0,1:T(8,128)}, u32[]{:S(2)}) copy-start(f32[7,3,512]{2,0,1:T(8,128)} %param.14) | copy-start | bytes 129028
  2.1 8.8 %copy-start.6 = (bf16[512,512]{1,0:T(8,128)(2,1)S(1)}, bf16[512,512]{1,0:T(8,128)(2,1)}, u32[]{:S(2)}) copy-start(bf16[512,512]{1,0:T(8,128)(2,1)} %param.12) | copy-start | bytes 1572868
  2.1 26.5 %copy-start.1 = (bf16[256,512]{1,0:T(8,128)(2,1)S(1)}, bf16[256,512]{1,0:T(8,128)(2,1)}, u32[]{:S(2)}) copy-start(bf16[256,512]{1,0:T(8,128)(2,1)} %constant.35.forward_hbm) | copy-start | bytes 786436
  2.1 26.5 %copy-start.2 = (f32[2,128,256]{2,1,0:T(8,128)S(1)}, f32[2,128,256]{2,1,0:T(8,128)}, u32[]{:S(2)}) copy-start(f32[2,128,256]{2,1,0:T(8,128)} %constant.31.clone.twist_hbm) | copy-start | bytes 786436
  2.1 26.5 %copy-start.3 = (bf16[512,256]{1,0:T(8,128)(2,1)S(1)}, bf16[512,256]{1,0:T(8,128)(2,1)}, u32[]{:S(2)}) copy-start(bf16[512,256]{1,0:T(8,128)(2,1)} %constant.38.backward_hbm) | copy-start | bytes 786436
  2.1 26.5 %copy-start.4 = (bf16[256,256]{1,0:T(8,128)(2,1)S(1)}, bf16[256,256]{1,0:T(8,128)(2,1)}, u32[]{:S(2)}) copy-start(bf16[256,256]{1,0:T(8,128)(2,1)} %constant.36.inward_hbm) | copy-start | bytes 393220
  2.1 26.5 %copy-start.5 = (bf16[256,256]{1,0:T(8,128)(2,1)S(1)}, bf16[256,256]{1,0:T(8,128)(2,1)}, u32[]{:S(2)}) copy-start(bf16[256,256]{1,0:T(8,128)(2,1)} %constant.37.outward_hbm) | copy-start | bytes 393220
  2.2 26.4 %all-to-all-start = ((bf16[32,8,2176]{2,1,0:T(8,128)(2,1)}), bf16[32,8,2176]{2,1,0:T(8,128)(2,1)S(1)}, u32[]{:S(2)}, u32[]{:S(2)}) async-start(bf16[32,8,2176]{2,1,0:T(8,128)(2,1)} %letters.1), calls=%async_computation | async-start | bytes 2228224 | tf_op jit(solution)/shard_map/all_to_all | solution.py:281
  11.1 6.9 %collective-permute-start.1 = (f32[1,512]{1,0:T(1,128)S(1)}, f32[1,512]{1,0:T(1,128)S(1)}, u32[]{:S(2)}, u32[]{:S(2)}) collective-permute-start(f32[1,512]{1,0:T(1,128)S(1)} %bitcast.9), channel_id=1, source_target_pairs={{7,0},{0,1},{1,2},{2,3},{3,4},{4,5},{5,6},{6,7},{15,8},{8,9},{9,10... | collective-permute-start | bytes 6152 | tf_op jit(solution)/shard_map/ppermute | solution.py:263
  12.8 5.2 %collective-permute-start = (f32[1,512]{1,0:T(1,128)S(1)}, f32[1,512]{1,0:T(1,128)S(1)}, u32[]{:S(2)}, u32[]{:S(2)}) collective-permute-start(f32[1,512]{1,0:T(1,128)S(1)} %bitcast.10), channel_id=1, source_target_pairs={{1,0},{2,1},{3,2},{4,3},{5,4},{6,5},{7,6},{0,7},{9,8},{10,9},{11,1... | collective-permute-start | bytes 6152 | tf_op jit(solution)/shard_map/ppermute | solution.py:263
  18.0 5.8 %collective-permute-start.3 = (f32[1,512]{1,0:T(1,128)S(1)}, f32[1,512]{1,0:T(1,128)S(1)}, u32[]{:S(2)}, u32[]{:S(2)}) collective-permute-start(f32[1,512]{1,0:T(1,128)S(1)} %get-tuple-element.6), channel_id=1, source_target_pairs={{5,0},{6,1},{7,2},{0,3},{1,4},{2,5},{3,6},{4,7},{13,8},{14,9},{15,... | collective-permute-start | bytes 6152 | tf_op jit(solution)/shard_map/ppermute | solution.py:263
  22.3 4.5 %collective-permute-start.2 = (f32[1,512]{1,0:T(1,128)S(1)}, f32[1,512]{1,0:T(1,128)S(1)}, u32[]{:S(2)}, u32[]{:S(2)}) collective-permute-start(f32[1,512]{1,0:T(1,128)S(1)} %get-tuple-element.5), channel_id=1, source_target_pairs={{3,0},{4,1},{5,2},{6,3},{7,4},{0,5},{1,6},{2,7},{11,8},{12,9},{13,... | collective-permute-start | bytes 6152 | tf_op jit(solution)/shard_map/ppermute | solution.py:263

commit v3 on v2

--- a/solution.py
+++ b/solution.py
@@ -178,8 +178,14 @@
         for i in range(0, STEP, CONV):
             convolve(block * STEP + i)
 
+    def transform_streams(start):
+        return transform([both_sides(gated, start + i).astype(bf16) for i in range(BATCH)])
+
+    following = transform_streams(0)
     for start in range(0, CHANNELS, BATCH):
-        streams = transform([both_sides(gated, start + i).astype(bf16) for i in range(BATCH)])
+        streams = following
+        if start + BATCH < CHANNELS:
+            following = transform_streams(start + BATCH)
         turned = []
         for i in range(BATCH):
             h_real, h_imag = h_hat[start + i, :LANES], h_hat[start + i, LANES:]

time: 68.9 us -> 68.9 us (level)
  no operation moved by 1% of the time
where the time goes in v3:
time: 68.9 us; the launch traced here: 68.6 us
  blocking collectives  25.5 us (37%)
  starting transfers between devices  19 us (28%)
  Pallas kernels  15.6 us (23%)
  waiting for transfers between devices  5.49 us (8%)
  local copies, waits for them, and re-layouts  1.95 us (3%)
  other arithmetic  0.99 us (1%)
    all_to_all x1, blocking collectives, shards(): return lax.all_to_all(mixed, 'seq', split_axis=0, concat_axis=0, tiled=True)  25.5 us
    pallas_call x1, Pallas kernels, mix_tokens(): pl.pallas_call(mixer_kernel, out_shape=jax.ShapeDtypeStruct((DEVICES * CH...  13.5 us
    ppermute x4, starting transfers between devices, arriving_from(): return lax.ppermute(x, axis, [((i + by) % size, i) for i in range(size)])  10.3 us
    all_to_all x1, starting transfers between devices, shards(): lax.all_to_all(letters, 'seq', split_axis=0, concat_axis=0, tiled=True)  8.73 us
    ppermute x4, waiting for transfers between devices, arriving_from(): return lax.ppermute(x, axis, [((i + by) % size, i) for i in range(size)])  4.59 us
    pallas_call x1, Pallas kernels, write_letters(): pl.pallas_call(letters_kernel, out_shape=jax.ShapeDtypeStruct((DEVICES, 8...  2.1 us
  transfers between devices with their start and end apart: 5, of which 4 were waited for; matrix products, arithmetic and copies ran while one was open for 3% of the time, Pallas kernels for 0%

profile of v3, /device:TPU:1, one launch (start us, length us, event | category | flops | bytes accessed | tf_op | source)
XLA Modules:
  0.0 68.6 jit_solution(16223398821059003204)
XLA Ops:
  0.0 0.0 copy-start
  0.0 2.1 %letters.1 = bf16[32,8,2176]{2,1,0:T(8,128)(2,1)} custom-call(bf16[32,2,8,1024]{3,2,1,0:T(8,128)(2,1)} %bitcast.8, s32[8,128]{1,0:T(8,128)} %bitcast.13), custom_call_target="tpu_custom_call" | custom-call | bytes 2097152 | tf_op jit(solution)/shard_map/letters/pallas_call | solution.py:250
  2.1 0.0 copy-start.6
  2.1 0.0 copy-start.1
  2.1 0.0 copy-start.2
  2.1 0.0 copy-start.3
  2.1 0.0 copy-start.4
  2.1 0.0 copy-start.5
  2.2 8.7 %all-to-all-start = ((bf16[32,8,2176]{2,1,0:T(8,128)(2,1)}), bf16[32,8,2176]{2,1,0:T(8,128)(2,1)S(1)}, u32[]{:S(2)}, u32[]{:S(2)}) async-start(bf16[32,8,2176]{2,1,0:T(8,128)(2,1)} %letters.1), calls=%async_computation | async-start | bytes 2228224 | tf_op jit(solution)/shard_map/all_to_all | solution.py:287
  10.9 0.0 copy-done.6
  10.9 0.2 multiply_reduce_fusion
  11.1 1.7 %collective-permute-start.1 = (f32[1,512]{1,0:T(1,128)S(1)}, f32[1,512]{1,0:T(1,128)S(1)}, u32[]{:S(2)}, u32[]{:S(2)}) collective-permute-start(f32[1,512]{1,0:T(1,128)S(1)} %bitcast.9), channel_id=1, source_target_pairs={{7,0},{0,1},{1,2},{2,3},{3,4},{4,5},{5,6},{6,7},{15,8},{8,9},{9,10... | collective-permute-start | bytes 6152 | tf_op jit(solution)/shard_map/ppermute | solution.py:269
  12.8 4.0 %collective-permute-start = (f32[1,512]{1,0:T(1,128)S(1)}, f32[1,512]{1,0:T(1,128)S(1)}, u32[]{:S(2)}, u32[]{:S(2)}) collective-permute-start(f32[1,512]{1,0:T(1,128)S(1)} %bitcast.10), channel_id=1, source_target_pairs={{1,0},{2,1},{3,2},{4,3},{5,4},{6,5},{7,6},{0,7},{9,8},{10,9},{11,1... | collective-permute-start | bytes 6152 | tf_op jit(solution)/shard_map/ppermute | solution.py:269
  16.8 1.2 %collective-permute-done.1 = f32[1,512]{1,0:T(1,128)S(1)} collective-permute-done((f32[1,512]{1,0:T(1,128)S(1)}, f32[1,512]{1,0:T(1,128)S(1)}, u32[]{:S(2)}, u32[]{:S(2)}) %collective-permute-start.1) | collective-permute-done | bytes 2080 | tf_op jit(solution)/shard_map/ppermute | solution.py:269
  18.0 0.0 collective-permute-done
  18.0 4.3 %collective-permute-start.3 = (f32[1,512]{1,0:T(1,128)S(1)}, f32[1,512]{1,0:T(1,128)S(1)}, u32[]{:S(2)}, u32[]{:S(2)}) collective-permute-start(f32[1,512]{1,0:T(1,128)S(1)} %get-tuple-element.6), channel_id=1, source_target_pairs={{5,0},{6,1},{7,2},{0,3},{1,4},{2,5},{3,6},{4,7},{13,8},{14,9},{15,... | collective-permute-start | bytes 6152 | tf_op jit(solution)/shard_map/ppermute | solution.py:269
  22.3 0.3 collective-permute-start.2
  22.5 0.0 copy-done
  22.5 0.1 constant_dynamic-slice_fusion
  22.6 0.8 %dynamic_slice.9.skip_ref = f32[16]{0:T(128)S(1)} dynamic-slice(f32[512]{0:T(512)} %param.16, s32[]{:T(128)S(6)} %select_n.2), dynamic_slice_sizes={16} | dynamic-slice | bytes 132 | tf_op jit(solution)/shard_map/dynamic_slice | solution.py:295
  23.4 0.4 collective-permute-done.3
  23.8 3.0 %collective-permute-done.2 = f32[1,512]{1,0:T(1,128)S(1)} collective-permute-done((f32[1,512]{1,0:T(1,128)S(1)}, f32[1,512]{1,0:T(1,128)S(1)}, u32[]{:S(2)}, u32[]{:S(2)}) %collective-permute-start.2) | collective-permute-done | bytes 2080 | tf_op jit(solution)/shard_map/ppermute | solution.py:269
  26.8 0.8 %multiply_convert_fusion.table_ref = bf16[3,16,512]{2,1,0:T(8,128)(2,1)S(1)} fusion(f32[512]{0:T(512)S(1)} %bitcast.12, bf16[3,512,512]{2,1,0:T(8,128)(2,1)} %param.13, s32[]{:T(128)S(6)} %select_n.2), kind=kLoop, calls=%fused_computation.1 | loop fusion | flops 73728 | bytes 100356 | tf_op jit(solution)/shard_map/convert_element_type | solution.py:291
  27.6 0.9 %all-to-all-done.mail_ref = bf16[32,8,2176]{2,1,0:T(8,128)(2,1)S(1)} async-done(((bf16[32,8,2176]{2,1,0:T(8,128)(2,1)}), bf16[32,8,2176]{2,1,0:T(8,128)(2,1)S(1)}, u32[]{:S(2)}, u32[]{:S(2)}) %all-to-all-start) | async-done | bytes 1114144 | tf_op jit(solution)/shard_map/all_to_all | solution.py:287
  28.5 0.1 broadcast_in_dim.13.taps_ref
  28.6 0.0 copy-done.1
  28.7 0.0 copy-done.2
  28.7 0.0 copy-done.3
  28.7 0.0 copy-done.4
  28.7 0.0 copy-done.5
  28.7 13.5 %mixer.1 = bf16[512,1024]{1,0:T(8,128)(2,1)S(1)} custom-call(f32[16]{0:T(128)S(1)} %dynamic_slice.9.skip_ref, bf16[32,8,2176]{2,1,0:T(8,128)(2,1)S(1)} %all-to-all-done.mail_ref, bf16[3,16,512]{2,1,0:T(8,128)(2,1)S(1)} %multiply_convert_fusion.table_ref, f32[21,16,128]{2,1,0:T(8,128)S(1)} %broadcast_in_dim.13.taps_ref, bf16[256,512]{1,0:T(8,128)(2,1)S(1)} %copy-done.1, ...), custom_call_target="tpu_custom_call" | custom-call | flops 4000000000 | bytes 4000000 | tf_op jit(solution)/shard_map/mixer/pallas_call | solution.py:217
  42.2 25.5 %all_to_all.17 = bf16[32,16,1024]{2,1,0:T(8,128)(2,1)S(1)} all-to-all(bf16[32,16,1024]{2,1,0:T(8,128)(2,1)S(1)} %bitcast.6), channel_id=1, replica_groups=mesh['seq'=32,'ch'=8] {'seq'}, dimensions={0} | all-to-all | bytes 2097152 | tf_op jit(solution)/shard_map/all_to_all | solution.py:298
  67.6 1.0 %copy.14 = bf16[512,1024]{1,0:T(8,128)(2,1)} copy(bf16[512,1024]{1,0:T(8,128)(2,1)S(1)} %bitcast.7) | data formatting | bytes 2097152
  (4 shorter events, 0.0 us)
Async XLA Ops:
  0.0 22.5 %copy-start = (f32[7,3,512]{2,0,1:T(8,128)S(1)}, f32[7,3,512]{2,0,1:T(8,128)}, u32[]{:S(2)}) copy-start(f32[7,3,512]{2,0,1:T(8,128)} %param.14) | copy-start | bytes 129028
  2.1 8.8 %copy-start.6 = (bf16[512,512]{1,0:T(8,128)(2,1)S(1)}, bf16[512,512]{1,0:T(8,128)(2,1)}, u32[]{:S(2)}) copy-start(bf16[512,512]{1,0:T(8,128)(2,1)} %param.12) | copy-start | bytes 1572868
  2.1 26.5 %copy-start.1 = (bf16[256,512]{1,0:T(8,128)(2,1)S(1)}, bf16[256,512]{1,0:T(8,128)(2,1)}, u32[]{:S(2)}) copy-start(bf16[256,512]{1,0:T(8,128)(2,1)} %constant.35.forward_hbm) | copy-start | bytes 786436
  2.1 26.5 %copy-start.2 = (f32[2,128,256]{2,1,0:T(8,128)S(1)}, f32[2,128,256]{2,1,0:T(8,128)}, u32[]{:S(2)}) copy-start(f32[2,128,256]{2,1,0:T(8,128)} %constant.31.clone.twist_hbm) | copy-start | bytes 786436
  2.1 26.5 %copy-start.3 = (bf16[512,256]{1,0:T(8,128)(2,1)S(1)}, bf16[512,256]{1,0:T(8,128)(2,1)}, u32[]{:S(2)}) copy-start(bf16[512,256]{1,0:T(8,128)(2,1)} %constant.38.backward_hbm) | copy-start | bytes 786436
  2.1 26.5 %copy-start.4 = (bf16[256,256]{1,0:T(8,128)(2,1)S(1)}, bf16[256,256]{1,0:T(8,128)(2,1)}, u32[]{:S(2)}) copy-start(bf16[256,256]{1,0:T(8,128)(2,1)} %constant.36.inward_hbm) | copy-start | bytes 393220
  2.1 26.5 %copy-start.5 = (bf16[256,256]{1,0:T(8,128)(2,1)S(1)}, bf16[256,256]{1,0:T(8,128)(2,1)}, u32[]{:S(2)}) copy-start(bf16[256,256]{1,0:T(8,128)(2,1)} %constant.37.outward_hbm) | copy-start | bytes 393220
  2.2 26.4 %all-to-all-start = ((bf16[32,8,2176]{2,1,0:T(8,128)(2,1)}), bf16[32,8,2176]{2,1,0:T(8,128)(2,1)S(1)}, u32[]{:S(2)}, u32[]{:S(2)}) async-start(bf16[32,8,2176]{2,1,0:T(8,128)(2,1)} %letters.1), calls=%async_computation | async-start | bytes 2228224 | tf_op jit(solution)/shard_map/all_to_all | solution.py:287
  11.1 6.9 %collective-permute-start.1 = (f32[1,512]{1,0:T(1,128)S(1)}, f32[1,512]{1,0:T(1,128)S(1)}, u32[]{:S(2)}, u32[]{:S(2)}) collective-permute-start(f32[1,512]{1,0:T(1,128)S(1)} %bitcast.9), channel_id=1, source_target_pairs={{7,0},{0,1},{1,2},{2,3},{3,4},{4,5},{5,6},{6,7},{15,8},{8,9},{9,10... | collective-permute-start | bytes 6152 | tf_op jit(solution)/shard_map/ppermute | solution.py:269
  12.8 5.2 %collective-permute-start = (f32[1,512]{1,0:T(1,128)S(1)}, f32[1,512]{1,0:T(1,128)S(1)}, u32[]{:S(2)}, u32[]{:S(2)}) collective-permute-start(f32[1,512]{1,0:T(1,128)S(1)} %bitcast.10), channel_id=1, source_target_pairs={{1,0},{2,1},{3,2},{4,3},{5,4},{6,5},{7,6},{0,7},{9,8},{10,9},{11,1... | collective-permute-start | bytes 6152 | tf_op jit(solution)/shard_map/ppermute | solution.py:269
  18.0 5.8 %collective-permute-start.3 = (f32[1,512]{1,0:T(1,128)S(1)}, f32[1,512]{1,0:T(1,128)S(1)}, u32[]{:S(2)}, u32[]{:S(2)}) collective-permute-start(f32[1,512]{1,0:T(1,128)S(1)} %get-tuple-element.6), channel_id=1, source_target_pairs={{5,0},{6,1},{7,2},{0,3},{1,4},{2,5},{3,6},{4,7},{13,8},{14,9},{15,... | collective-permute-start | bytes 6152 | tf_op jit(solution)/shard_map/ppermute | solution.py:269
  22.3 4.5 %collective-permute-start.2 = (f32[1,512]{1,0:T(1,128)S(1)}, f32[1,512]{1,0:T(1,128)S(1)}, u32[]{:S(2)}, u32[]{:S(2)}) collective-permute-start(f32[1,512]{1,0:T(1,128)S(1)} %get-tuple-element.5), channel_id=1, source_target_pairs={{3,0},{4,1},{5,2},{6,3},{7,4},{0,5},{1,6},{2,7},{11,8},{12,9},{13,... | collective-permute-start | bytes 6152 | tf_op jit(solution)/shard_map/ppermute | solution.py:269
